TPU v7x, 32 devices: a whole 2x2x4 slice. The times are simulated.
32 devices in a mesh: wide: 16 (over z, y, x), narrow: 2 (over core).
Axes of the slice: x: 2, y: 2, z: 4, core: 2. Of those that a mesh axis runs over, the one named last changes fastest.
Arguments:
- latent_tokens: float32 [384, 16384], P('narrow', 'wide'), may hold values from -52 to 52
- labels: int32 [64], P('wide'), may hold values from 0 to 1000
- timesteps: int32 [64], P('wide'), may hold values from 0 to 999
- class_table: bfloat16 [1001, 384], replicated, may hold values from -6 to 6
- modulation_weight: bfloat16 [384, 6, 384], P('wide', None, 'narrow'), may hold values from -0.3125 to 0.3125
- modulation_bias: float32 [6, 384], P(None, 'narrow'), may hold values from -3 to 3
- in_weight: bfloat16 [384, 3, 384], P('wide', None, 'narrow'), may hold values from -0.21875 to 0.21875
- in_bias: float32 [2, 384], P(None, 'narrow'), may hold values from -3 to 3
- out_weight: bfloat16 [384, 384], P('narrow', 'wide'), may hold values from -1.25 to 1.25
- out_bias: float32 [384], P('narrow'), may hold values from -3 to 3
- up_weight: bfloat16 [384, 1536], P('wide', 'narrow'), may hold values from -0.3125 to 0.3125
- up_bias: float32 [1536], P('narrow'), may hold values from -3 to 3
- down_weight: bfloat16 [1536, 384], P('narrow', 'wide'), may hold values from -0.3125 to 0.3125
- down_bias: float32 [384], P('narrow'), may hold values from -3 to 3
- cotangent: float32 [384, 16384], P('narrow', 'wide'), may hold values from -6 to 6
Outputs:
- block_output: float32 [384, 16384], P('narrow', 'wide')
- token_grads: float32 [384, 16384], P('narrow', 'wide')
- condition_grads: float32 [64, 384], P('wide')
- table_grads: float32 [1001, 384], replicated
- modulation_grads: float32 [384, 6, 384], P('wide', None, 'narrow')
- modulation_bias_grads: float32 [6, 384], P(None, 'narrow')
- in_grads: float32 [384, 3, 384], P('wide', None, 'narrow')
- in_bias_grads: float32 [2, 384], P(None, 'narrow')
- out_grads: float32 [384, 384], P('narrow', 'wide')
- out_bias_grads: float32 [384], P('narrow')
- up_grads: float32 [384, 1536], P('wide', 'narrow')
- up_bias_grads: float32 [1536], P('narrow')
- down_grads: float32 [1536, 384], P('narrow', 'wide')
- down_bias_grads: float32 [384], P('narrow')
All inputs are finite; a program needn't handle non-finite values.
Results may differ from a plain program's by a relative error of at most 0.017.
Values may be sent and summed in bfloat16 or wider, within the bound.
A program may use at most 128 MiB of HBM per device.

v0:
```python
import math

import jax
import jax.numpy as jnp
from jax import lax
from jax.sharding import PartitionSpec as P

D = 384
HD = 64


EPS = 1e-06
GELU_K = 0.7978845608028654
GELU_A = 0.044715


def time_features(timesteps):
    half_width = D // 2
    frequencies = jnp.exp(
        jnp.arange(half_width, dtype=jnp.float32) * (-math.log(10000.0) / half_width)
    )
    angles = timesteps.astype(jnp.float32)[:, None] * frequencies[None, :]
    return jnp.concatenate([jnp.cos(angles), jnp.sin(angles)], axis=1)


def gelu_value(inputs):
    inner = GELU_K * (inputs + GELU_A * inputs * inputs * inputs)
    return 0.5 * inputs * (1.0 + jnp.tanh(inner))


def gelu_slope(inputs):
    inner = GELU_K * (inputs + GELU_A * inputs * inputs * inputs)
    tangent = jnp.tanh(inner)
    return 0.5 * (1.0 + tangent) + 0.5 * inputs * (1.0 - tangent * tangent) * GELU_K * (
        1.0 + 3.0 * GELU_A * inputs * inputs
    )


def silu_slope(inputs):
    sigmoid = jax.nn.sigmoid(inputs)
    return sigmoid * (1.0 + inputs * (1.0 - sigmoid))


def feature_totals(first, second):
    return lax.psum(
        (jnp.sum(first, axis=-1, keepdims=True), jnp.sum(second, axis=-1, keepdims=True)), "narrow"
    )


def norm_forward(values):
    total, squares = feature_totals(values, values * values)
    average = total / D
    inv_std = lax.rsqrt(squares / D - average * average + EPS)
    return ((values - average) * inv_std, inv_std)


def norm_backward(grad_norm, normed, inv_std):
    first, second = feature_totals(grad_norm, grad_norm * normed)
    return inv_std * (grad_norm - first / D - normed * (second / D))


def modulate_back(grad_mod, normed, scale):
    return (jnp.sum(grad_mod, axis=1), jnp.sum(grad_mod * normed, axis=1), grad_mod * (1.0 + scale))


def spread_features(half_rows):
    return lax.all_gather(half_rows, "narrow", axis=2, tiled=True)


def branch_total(partial_value):
    return lax.psum_scatter(
        partial_value.astype(jnp.bfloat16), "narrow", scatter_dimension=2, tiled=True
    ).astype(jnp.float32)


def spread_grads(half_rows):
    return lax.all_gather(half_rows, "narrow", axis=2, tiled=True)


def input_total(partial_value):
    return lax.psum_scatter(
        partial_value.astype(jnp.bfloat16), "narrow", scatter_dimension=2, tiled=True
    ).astype(jnp.float32)


def shards(
    latent_tokens,
    labels,
    timesteps,
    class_table,
    modulation_weight,
    modulation_bias,
    in_weight,
    in_bias,
    out_weight,
    out_bias,
    up_weight,
    up_bias,
    down_weight,
    down_bias,
    cotangent,
):
    latent_count = labels.shape[0]
    half_width = latent_tokens.shape[0]
    local_tokens = latent_tokens.shape[1]
    sequence = local_tokens // latent_count
    head_count = half_width // HD
    head_shape = (latent_count, sequence, head_count, HD)
    score_scale = HD ** (-0.5)
    weight_scale = (local_tokens * lax.axis_size("wide")) ** (-0.5)
    modulation_full, in_full, out_full, up_full, down_full = (
        lax.all_gather(modulation_weight, "wide", axis=0, tiled=True),
        lax.all_gather(in_weight, "wide", axis=0, tiled=True),
        lax.all_gather(out_weight, "wide", axis=1, tiled=True),
        lax.all_gather(up_weight, "wide", axis=0, tiled=True),
        lax.all_gather(down_weight, "wide", axis=1, tiled=True),
    )
    class_ids = jnp.arange(class_table.shape[0], dtype=jnp.int32)
    one_hot = (labels[:, None] == class_ids[None, :]).astype(jnp.float32)
    condition = jnp.dot(
        one_hot.astype(jnp.bfloat16), class_table, preferred_element_type=jnp.float32
    ) + time_features(timesteps)
    activated = jax.nn.silu(condition).astype(jnp.bfloat16)
    modulation = (
        jnp.einsum("bd,djf->bjf", activated, modulation_full, preferred_element_type=jnp.float32)
        + modulation_bias
    )
    shift_one, scale_one, gate_one, shift_two, scale_two, gate_two = [
        modulation[:, which][:, None, :] for which in range(6)
    ]
    hidden_in = jnp.transpose(latent_tokens).reshape(latent_count, sequence, half_width)
    upstream = jnp.transpose(cotangent).reshape(latent_count, sequence, half_width)
    normed_one, inv_one = norm_forward(hidden_in)
    modulated_one = spread_features(
        (normed_one * (1.0 + scale_one) + shift_one).astype(jnp.bfloat16)
    )
    projected = jnp.einsum(
        "bsd,djf->bsjf", modulated_one, in_full, preferred_element_type=jnp.float32
    )
    queries = (projected[:, :, 0] + in_bias[0]).astype(jnp.bfloat16).reshape(head_shape)
    key_rows = projected[:, :, 1].astype(jnp.bfloat16).reshape(head_shape)
    value_rows = (projected[:, :, 2] + in_bias[1]).astype(jnp.bfloat16).reshape(head_shape)
    scores = (
        jnp.einsum("bshe,bthe->bhst", queries, key_rows, preferred_element_type=jnp.float32)
        * score_scale
    )
    log_total = jnp.log(jnp.sum(jnp.exp(scores), axis=-1, keepdims=True))
    mixing = jnp.exp(scores - log_total).astype(jnp.bfloat16)
    attended = jnp.einsum("bhst,bthe->bshe", mixing, value_rows, preferred_element_type=jnp.float32)
    attended = attended.astype(jnp.bfloat16).reshape(latent_count, sequence, half_width)
    attention = (
        branch_total(
            jnp.einsum("bsd,de->bse", attended, out_full, preferred_element_type=jnp.float32)
        )
        + out_bias
    )
    middle = hidden_in + gate_one * attention
    normed_two, inv_two = norm_forward(middle)
    modulated_two = spread_features(
        (normed_two * (1.0 + scale_two) + shift_two).astype(jnp.bfloat16)
    )
    pre_act = (
        jnp.einsum("bsd,df->bsf", modulated_two, up_full, preferred_element_type=jnp.float32)
        + up_bias
    )
    activation = gelu_value(pre_act).astype(jnp.bfloat16)
    feedforward = (
        branch_total(
            jnp.einsum("bsf,fd->bsd", activation, down_full, preferred_element_type=jnp.float32)
        )
        + down_bias
    )
    block_output = middle + gate_two * feedforward
    modulation_full, in_full, out_full, up_full, down_full = (
        lax.all_gather(modulation_weight, "wide", axis=0, tiled=True),
        lax.all_gather(in_weight, "wide", axis=0, tiled=True),
        lax.all_gather(out_weight, "wide", axis=1, tiled=True),
        lax.all_gather(up_weight, "wide", axis=0, tiled=True),
        lax.all_gather(down_weight, "wide", axis=1, tiled=True),
    )
    gate_two_grad = jnp.sum(upstream * feedforward, axis=1)
    grad_ff = gate_two * upstream
    grad_ff_full = spread_grads(grad_ff.astype(jnp.bfloat16))
    down_total = jnp.einsum(
        "bsf,bsd->fd", activation, grad_ff_full, preferred_element_type=jnp.float32
    )
    grad_pre = jnp.einsum(
        "bsd,fd->bsf", grad_ff_full, down_full, preferred_element_type=jnp.float32
    ) * gelu_slope(pre_act)
    grad_pre_bf = grad_pre.astype(jnp.bfloat16)
    up_total = jnp.einsum(
        "bsd,bsf->df", modulated_two, grad_pre_bf, preferred_element_type=jnp.float32
    )
    grad_mod_two = input_total(
        jnp.einsum("bsf,df->bsd", grad_pre_bf, up_full, preferred_element_type=jnp.float32)
    )
    shift_two_grad, scale_two_grad, grad_norm_two = modulate_back(
        grad_mod_two, normed_two, scale_two
    )
    grad_middle = upstream + norm_backward(grad_norm_two, normed_two, inv_two)
    gate_one_grad = jnp.sum(grad_middle * attention, axis=1)
    grad_att = gate_one * grad_middle
    grad_att_full = spread_grads(grad_att.astype(jnp.bfloat16))
    out_total = jnp.einsum(
        "bsd,bse->de", attended, grad_att_full, preferred_element_type=jnp.float32
    )
    grad_attended = jnp.einsum(
        "bse,de->bsd", grad_att_full, out_full, preferred_element_type=jnp.float32
    )
    grad_attended = grad_attended.astype(jnp.bfloat16).reshape(head_shape)
    scores_again = (
        jnp.einsum("bshe,bthe->bhst", queries, key_rows, preferred_element_type=jnp.float32)
        * score_scale
    )
    weights_full = jnp.exp(scores_again - log_total)
    grad_mixing = jnp.einsum(
        "bshe,bthe->bhst", grad_attended, value_rows, preferred_element_type=jnp.float32
    )
    row_dots = jnp.sum(weights_full * grad_mixing, axis=-1, keepdims=True)
    grad_scores = (weights_full * (grad_mixing - row_dots) * score_scale).astype(jnp.bfloat16)
    flat_shape = (latent_count, sequence, half_width)
    grad_queries = jnp.einsum(
        "bhst,bthe->bshe", grad_scores, key_rows, preferred_element_type=jnp.float32
    ).reshape(flat_shape)
    grad_keys = jnp.einsum(
        "bhst,bshe->bthe", grad_scores, queries, preferred_element_type=jnp.float32
    ).reshape(flat_shape)
    grad_values = jnp.einsum(
        "bhst,bshe->bthe", mixing, grad_attended, preferred_element_type=jnp.float32
    ).reshape(flat_shape)
    grad_proj = jnp.stack([grad_queries, grad_keys, grad_values], axis=2).astype(jnp.bfloat16)
    in_total = jnp.einsum(
        "bsd,bsjf->djf", modulated_one, grad_proj, preferred_element_type=jnp.float32
    )
    grad_mod_one = input_total(
        jnp.einsum("bsjf,djf->bsd", grad_proj, in_full, preferred_element_type=jnp.float32)
    )
    shift_one_grad, scale_one_grad, grad_norm_one = modulate_back(
        grad_mod_one, normed_one, scale_one
    )
    token_grads = grad_middle + norm_backward(grad_norm_one, normed_one, inv_one)
    grad_modulation = jnp.stack(
        [
            shift_one_grad,
            scale_one_grad,
            gate_one_grad,
            shift_two_grad,
            scale_two_grad,
            gate_two_grad,
        ],
        axis=1,
    )
    grad_modulation_bf = grad_modulation.astype(jnp.bfloat16)
    modulation_total = jnp.einsum(
        "bd,bjf->djf", activated, grad_modulation_bf, preferred_element_type=jnp.float32
    )
    grad_activated = lax.psum(
        jnp.einsum(
            "bjf,djf->bd", grad_modulation_bf, modulation_full, preferred_element_type=jnp.float32
        ),
        "narrow",
    )
    condition_grads = grad_activated * silu_slope(condition) * sequence ** (-0.5)
    in_bias_part = jnp.stack(
        [jnp.sum(grad_queries, axis=(0, 1)), jnp.sum(grad_values, axis=(0, 1))]
    )
    every_label = lax.all_gather(labels, "wide", axis=0, tiled=True)
    every_row = lax.all_gather(condition_grads, "wide", axis=0, tiled=True)
    every_hot = (every_label[:, None] == class_ids[None, :]).astype(jnp.float32)
    table_grads = jnp.einsum("bc,bd->cd", every_hot, every_row, precision=lax.Precision.HIGHEST)
    modulation_bias_sum, in_bias_sum, out_bias_sum, up_bias_sum, down_bias_sum = lax.psum(
        (
            jnp.sum(grad_modulation, axis=0),
            in_bias_part,
            jnp.sum(grad_att, axis=(0, 1)),
            jnp.sum(grad_pre, axis=(0, 1)),
            jnp.sum(grad_ff, axis=(0, 1)),
        ),
        "wide",
    )
    modulation_part, in_part, out_part, up_part, down_part = (
        lax.psum_scatter(modulation_total, "wide", scatter_dimension=0, tiled=True),
        lax.psum_scatter(in_total, "wide", scatter_dimension=0, tiled=True),
        lax.psum_scatter(out_total, "wide", scatter_dimension=1, tiled=True),
        lax.psum_scatter(up_total, "wide", scatter_dimension=0, tiled=True),
        lax.psum_scatter(down_total, "wide", scatter_dimension=1, tiled=True),
    )
    return (
        jnp.transpose(block_output.reshape(-1, half_width)),
        jnp.transpose(token_grads.reshape(-1, half_width)),
        condition_grads,
        table_grads,
        modulation_part * weight_scale,
        modulation_bias_sum * weight_scale,
        in_part * weight_scale,
        in_bias_sum * weight_scale,
        out_part * weight_scale,
        out_bias_sum * weight_scale,
        up_part * weight_scale,
        up_bias_sum * weight_scale,
        down_part * weight_scale,
        down_bias_sum * weight_scale,
    )


def solution(mesh):
    return jax.shard_map(
        shards,
        mesh=mesh,
        in_specs=(
            P("narrow", "wide"),
            P("wide"),
            P("wide"),
            P(),
            P("wide", None, "narrow"),
            P(None, "narrow"),
            P("wide", None, "narrow"),
            P(None, "narrow"),
            P("narrow", "wide"),
            P("narrow"),
            P("wide", "narrow"),
            P("narrow"),
            P("narrow", "wide"),
            P("narrow"),
            P("narrow", "wide"),
        ),
        out_specs=(
            P("narrow", "wide"),
            P("narrow", "wide"),
            P("wide", None),
            P(),
            P("wide", None, "narrow"),
            P(None, "narrow"),
            P("wide", None, "narrow"),
            P(None, "narrow"),
            P("narrow", "wide"),
            P("narrow"),
            P("wide", "narrow"),
            P("narrow"),
            P("narrow", "wide"),
            P("narrow"),
        ),
        check_vma=False,
    )
```

profile of v0, /device:TPU:9, one launch (start us, length us, event | category | flops | bytes accessed | tf_op | source)
XLA Modules:
  0.0 991.6 jit_solution(11478589560562920146)
XLA Ops:
  7.3 36.9 %all_gather.38 = bf16[384,6,192]{2,0,1:T(8,128)(2,1)S(1)} all-gather(bf16[24,6,192]{2,0,1:T(8,128)(2,1)} %param.19), channel_id=1, replica_groups=mesh['wide'=16,'narrow'=2] {'wide'}, dimensions={0}, use_global_device_ids=true | all-gather | bytes 940032 | tf_op jit(solution)/shard_map/all_gather | solution.py:112
  47.7 8.3 all-reduce.5
  56.2 2.4 all_gather.39
  58.6 32.4 %all_gather.40 = bf16[384,3,192]{2,0,1:T(8,128)(2,1)S(1)} all-gather(bf16[24,3,192]{2,0,1:T(8,128)(2,1)S(1)} %copy-done.21), channel_id=1, replica_groups=mesh['wide'=16,'narrow'=2] {'wide'}, dimensions={0}, use_global_device_ids=true | all-gather | bytes 470016 | tf_op jit(solution)/shard_map/all_gather | solution.py:113
  91.8 1.0 fusion.108
  95.0 33.8 %all_gather.41 = bf16[192,384]{0,1:T(8,128)(2,1)} all-gather(bf16[192,24]{0,1:T(8,128)(2,1)} %param.23), channel_id=1, replica_groups=mesh['wide'=16,'narrow'=2] {'wide'}, dimensions={1}, use_global_device_ids=true | all-gather | bytes 156672 | tf_op jit(solution)/shard_map/all_gather | solution.py:114
  129.7 3.3 fusion.116
  133.0 4.8 convolution_convert_fusion.4
  137.8 2.3 convolution_convert_fusion.2
  140.2 35.6 %all_gather.43 = bf16[384,768]{1,0:T(8,128)(2,1)} all-gather(bf16[24,768]{1,0:T(8,128)(2,1)} %param.25), channel_id=1, replica_groups=mesh['wide'=16,'narrow'=2] {'wide'}, dimensions={0}, use_global_device_ids=true | all-gather | bytes 626688 | tf_op jit(solution)/shard_map/all_gather | solution.py:115
  175.8 36.1 %all_gather.44 = bf16[768,384]{0,1:T(8,128)(2,1)} all-gather(bf16[768,24]{0,1:T(8,128)(2,1)} %param.27), channel_id=1, replica_groups=mesh['wide'=16,'narrow'=2] {'wide'}, dimensions={1}, use_global_device_ids=true | all-gather | bytes 626688 | tf_op jit(solution)/shard_map/all_gather | solution.py:116
  212.0 1.3 fusion.106
  213.3 30.1 %all-reduce.4 = (f32[4,256,1]{1,0,2:T(4,128)}, f32[4,256,1]{1,0,2:T(4,128)}) all-reduce(f32[4,256,1]{1,0,2:T(4,128)S(1)} %bitcast.222, f32[4,256,1]{1,0,2:T(4,128)S(1)} %bitcast.221), channel_id=1, replica_groups=mesh['wide'=16,'narrow'=2] {'narrow'}, use_global_device_ids=true, to_apply=%region_9.10 | all-reduce | flops 2048 | bytes 16384 | tf_op jit(solution)/shard_map/psum | solution.py:45
  245.1 2.4 all_gather.42
  247.4 4.7 multiply_convert_fusion.1
  252.1 1.1 copy-done.37
  253.3 1.7 convolution_convert_fusion.1
  255.0 11.0 %reduce-scatter.12.cloned.1.call-done = bf16[4,256,192]{1,2,0:T(8,128)(2,1)} async-done(((bf16[4,256,384]{1,2,0:T(8,128)(2,1)}), bf16[4,256,192]{1,2,0:T(8,128)(2,1)}) %reduce-scatter.12.cloned.1.call-update) | async-done | bytes 393232 | tf_op jit(solution)/shard_map/reduce_scatter | solution.py:71
  266.0 2.2 fusion.49
  268.2 2.4 all_gather.45
  270.6 5.2 fusion.115
  275.8 1.2 copy-done.38
  277.0 1.7 convolution_convert_fusion
  279.0 4.6 fusion.8
  283.6 4.6 reduce-scatter.14.cloned.1.call-done
  288.2 2.2 fusion.46
  290.4 3.2 all-reduce.3
  294.2 3.8 multiply_reduce_fusion.3
  299.1 2.4 all_gather.46
  301.5 1.2 convolution_convert_fusion.3
  302.7 4.9 fusion.110
  307.6 3.6 fusion.80
  311.2 6.4 fusion.28
  317.6 6.4 fusion.109
  323.9 3.1 bitcast_convert_fusion
  327.1 2.1 convolution_bitcast_fusion.4
  329.3 3.5 convolution_bitcast_fusion.2
  332.9 3.2 convolution_bitcast_fusion.1
  337.0 1.2 mul.330.clone
  338.1 1.0 copy.81
  339.2 1.2 dynamic-slice
  341.3 10.2 %all-reduce = s32[64]{0:T(128)} all-reduce(s32[64]{0:T(128)S(1)} %dynamic-update-slice), channel_id=1, replica_groups=mesh['wide'=16,'narrow'=2] {'wide'}, use_global_device_ids=true, to_apply=%add | all-reduce | flops 64 | bytes 512
  351.6 1.8 fusion.54
  354.7 3.3 convolution_bitcast_fusion
  358.2 2.2 fusion.47
  360.5 1.9 fusion.83
  362.4 1.4 pad_maximum_fusion.3
  363.8 2.1 copy.79
  365.9 96.9 %reduce-scatter.22.cloned.1.call-done = f32[192,24]{0,1:T(8,128)} async-done(((f32[192,384]{0,1:T(8,128)}), f32[192,24]{0,1:T(8,128)}) %reduce-scatter.22.cloned.1.call-update) | async-done | bytes 18448 | tf_op jit(solution)/shard_map/reduce_scatter | solution.py:284
  462.8 1.3 broadcast_multiply_fusion.4
  464.1 127.8 %reduce-scatter.24.cloned.1.call-done = f32[24,768]{1,0:T(8,128)} async-done(((f32[384,768]{1,0:T(8,128)}), f32[24,768]{1,0:T(8,128)}) %reduce-scatter.24.cloned.1.call-update) | async-done | bytes 73744 | tf_op jit(solution)/shard_map/reduce_scatter | solution.py:285
  592.0 1.5 broadcast_multiply_fusion.2
  593.5 127.9 %reduce-scatter.26.cloned.1.call-done = f32[768,24]{0,1:T(8,128)} async-done(((f32[768,384]{0,1:T(8,128)}), f32[768,24]{0,1:T(8,128)}) %reduce-scatter.26.cloned.1.call-update) | async-done | bytes 73744 | tf_op jit(solution)/shard_map/reduce_scatter | solution.py:286
  721.4 1.5 broadcast_multiply_fusion.1
  723.6 1.0 convolution_bitcast_fusion.5
  724.6 6.5 all-reduce.2
  731.1 1.3 fusion.40
  733.5 26.7 %all-gather = f32[16,4,384]{2,1,0:T(4,128)S(1)} all-gather(f32[1,4,384]{2,1,0:T(4,128)S(1)} %bitcast.216), channel_id=1, replica_groups=mesh['wide'=16,'narrow'=2] {'wide'}, dimensions={0}, use_global_device_ids=true | all-gather | bytes 104448 | tf_op jit(solution)/shard_map/all_gather | solution.py:268
  760.2 57.3 %all-reduce.1 = (f32[6,192]{1,0:T(8,128)S(1)}, f32[2,192]{1,0:T(2,128)S(1)}, f32[192]{0:T(256)S(1)}, f32[768]{0:T(1024)S(1)}, f32[192]{0:T(256)S(1)}) all-reduce(f32[6,192]{1,0:T(8,128)S(1)} %copy-done.22, f32[2,192]{1,0:T(2,128)S(1)} %copy-done.30, f32[192]{0:T(256)S(1)} %copy-done.31, ...), channel_id=1, replica_groups=mesh['wide'=16,'narrow'=2] {'wide'}, use_global_device_ids=true, to_apply=%region_31.32 | all-reduce | flops 2688 | bytes 21504 | tf_op jit(solution)/shard_map/psum | solution.py:271
  820.5 2.0 fusion.77
  822.5 27.9 %reduce-scatter.20.cloned.1.call-done = f32[24,3,192]{2,0,1:T(8,128)} async-done(((f32[384,3,192]{2,0,1:T(8,128)}), f32[24,3,192]{2,0,1:T(8,128)}) %reduce-scatter.20.cloned.1.call-update) | async-done | bytes 55312 | tf_op jit(solution)/shard_map/reduce_scatter | solution.py:283
  850.4 1.5 broadcast_multiply_fusion.3
  851.9 131.5 %reduce-scatter.18.cloned.1.call-done = f32[24,6,192]{2,0,1:T(8,128)} async-done(((f32[384,6,192]{2,0,1:T(8,128)}), f32[24,6,192]{2,0,1:T(8,128)}) %reduce-scatter.18.cloned.1.call-update) | async-done | bytes 110608 | tf_op jit(solution)/shard_map/reduce_scatter | solution.py:282
  983.5 1.6 broadcast_multiply_fusion
  (140 shorter events, 18.8 us)
Async XLA Ops:
  7.2 37.8 %copy-start = (bf16[1001,384]{1,0:T(8,128)(2,1)S(1)}, bf16[1001,384]{1,0:T(8,128)(2,1)}, u32[]{:S(2)}) copy-start(bf16[1001,384]{1,0:T(8,128)(2,1)} %param.18) | copy-start | bytes 2306308
  7.2 40.3 %copy-start.1 = (f32[192,1024]{1,0:T(8,128)S(1)}, f32[192,1024]{1,0:T(8,128)}, u32[]{:S(2)}) copy-start(f32[192,1024]{1,0:T(8,128)} %param.15) | copy-start | bytes 2359300
  7.2 204.8 %reduce-scatter.10.cloned.1.call-start = ((), (), s32[]{:S(2)}) async-start(), calls=%async_computation.9 | async-start | bytes 1179648 | tf_op jit(solution)/shard_map/reduce_scatter | solution.py:71
  44.2 14.4 %copy-start.21 = (bf16[24,3,192]{2,0,1:T(8,128)(2,1)S(1)}, bf16[24,3,192]{2,0,1:T(8,128)(2,1)}, u32[]{:S(2)}) copy-start(bf16[24,3,192]{2,0,1:T(8,128)(2,1)} %param.21) | copy-start | bytes 82948
  45.9 1.6 copy-start.15
  55.9 302.2 %copy-start.18 = (f32[4,256]{1,0:T(4,128)}, f32[4,256]{1,0:T(4,128)S(1)}, u32[]{:S(2)}) copy-start(f32[4,256]{1,0:T(4,128)S(1)} %get-tuple-element.61) | copy-start | bytes 12292
  55.9 302.2 %copy-start.19 = (f32[4,256]{1,0:T(4,128)}, f32[4,256]{1,0:T(4,128)S(1)}, u32[]{:S(2)}) copy-start(f32[4,256]{1,0:T(4,128)S(1)} %get-tuple-element.62) | copy-start | bytes 12292
  58.6 34.2 %copy-start.5 = (bf16[4,256,384]{1,2,0:T(8,128)(2,1)}, bf16[4,256,384]{1,2,0:T(8,128)(2,1)S(1)}, u32[]{:S(2)}) copy-start(bf16[4,256,384]{1,2,0:T(8,128)(2,1)S(1)} %all_gather.39) | copy-start | bytes 2359300
  91.0 1.9 copy-start.7
  91.0 2.6 copy-start.34
  95.0 42.7 %copy-start.28 = (f32[3,64]{1,0:T(4,128)}, f32[3,64]{1,0:T(4,128)S(1)}, u32[]{:S(2)}) copy-start(f32[3,64]{1,0:T(4,128)S(1)} %add.180) | copy-start | bytes 2308
  128.9 0.7 copy-start.9
  129.0 4.0 copy-start.6
  140.1 125.8 %reduce-scatter.12.cloned.1.call-start = ((), (), s32[]{:S(2)}) async-start(), calls=%async_computation.10 | async-start | bytes 1179648 | tf_op jit(solution)/shard_map/reduce_scatter | solution.py:71
  247.4 4.7 copy-start.10
  247.4 5.8 copy-start.14
  252.1 1.1 copy-start.37
  255.0 33.2 %reduce-scatter.14.cloned.1.call-start = ((), (), s32[]{:S(2)}) async-start(), calls=%async_computation.11 | async-start | bytes 1179648 | tf_op jit(solution)/shard_map/reduce_scatter | solution.py:81
  270.6 5.2 copy-start.11
  270.6 6.5 copy-start.13
  275.8 1.2 copy-start.38
  278.7 79.4 %reduce-scatter.16.cloned.1.call-start = ((), (), s32[]{:S(2)}) async-start(), calls=%async_computation.12 | async-start | bytes 1179648 | tf_op jit(solution)/shard_map/reduce_scatter | solution.py:81
  294.2 7.3 copy-start.8
  298.0 0.9 copy-start.3
  301.5 6.1 copy-start.29
  327.1 135.7 %reduce-scatter.22.cloned.1.call-start = ((), (), s32[]{:S(2)}) async-start(), calls=%async_computation.15 | async-start | bytes 417792 | tf_op jit(solution)/shard_map/reduce_scatter | solution.py:284
  329.2 3.6 copy-start.12
  329.3 262.7 %reduce-scatter.24.cloned.1.call-start = ((), (), s32[]{:S(2)}) async-start(), calls=%async_computation.16 | async-start | bytes 1253376 | tf_op jit(solution)/shard_map/reduce_scatter | solution.py:285
  332.8 3.4 copy-start.20
  332.8 388.6 %reduce-scatter.26.cloned.1.call-start = ((), (), s32[]{:S(2)}) async-start(), calls=%async_computation.17 | async-start | bytes 1253376 | tf_op jit(solution)/shard_map/reduce_scatter | solution.py:286
  336.1 5.0 copy-start.36
  336.1 15.4 %copy-start.2 = (f32[192,1024]{1,0:T(8,128)S(1)}, f32[192,1024]{1,0:T(8,128)}, u32[]{:S(2)}) copy-start(f32[192,1024]{1,0:T(8,128)} %param.29) | copy-start | bytes 2359300
  336.2 514.2 %reduce-scatter.20.cloned.1.call-start = ((), (), s32[]{:S(2)}) async-start(), calls=%async_computation.14 | async-start | bytes 1253376 | tf_op jit(solution)/shard_map/reduce_scatter | solution.py:283
  354.7 5.7 copy-start.27
  354.7 5.7 copy-start.26
  354.7 5.7 copy-start.25
  354.7 5.7 copy-start.24
  354.7 5.8 copy-start.16
  358.1 625.4 %reduce-scatter.18.cloned.1.call-start = ((), (), s32[]{:S(2)}) async-start(), calls=%async_computation.13 | async-start | bytes 2506752 | tf_op jit(solution)/shard_map/reduce_scatter | solution.py:282
  362.4 368.7 %copy-start.4 = (f32[4,256,192]{1,2,0:T(8,128)S(1)}, f32[4,256,192]{1,2,0:T(8,128)}, u32[]{:S(2)}) copy-start(f32[4,256,192]{1,2,0:T(8,128)} %copy-done.3) | copy-start | bytes 2359300
  724.6 8.8 copy-start.17
  724.6 35.6 %copy-start.22 = (f32[6,192]{1,0:T(8,128)S(1)}, f32[6,192]{1,0:T(8,128)}, u32[]{:S(2)}) copy-start(f32[6,192]{1,0:T(8,128)} %reduce_sum.214) | copy-start | bytes 13828
  724.6 35.6 %copy-start.30 = (f32[2,192]{1,0:T(2,128)S(1)}, f32[2,192]{1,0:T(2,128)}, u32[]{:S(2)}) copy-start(f32[2,192]{1,0:T(2,128)} %pad_maximum_fusion.3) | copy-start | bytes 4612
  724.6 35.6 %copy-start.31 = (f32[192]{0:T(256)S(1)}, f32[192]{0:T(256)}, u32[]{:S(2)}) copy-start(f32[192]{0:T(256)} %get-tuple-element.18) | copy-start | bytes 2308
  724.6 35.6 %copy-start.32 = (f32[768]{0:T(1024)S(1)}, f32[768]{0:T(1024)}, u32[]{:S(2)}) copy-start(f32[768]{0:T(1024)} %get-tuple-element.69) | copy-start | bytes 9220
  724.6 35.6 %copy-start.33 = (f32[192]{0:T(256)S(1)}, f32[192]{0:T(256)}, u32[]{:S(2)}) copy-start(f32[192]{0:T(256)} %fusion.54) | copy-start | bytes 2308
  724.6 95.8 %copy-start.35 = (s32[64]{0:T(128)S(1)}, s32[64]{0:T(128)}, u32[]{:S(2)}) copy-start(s32[64]{0:T(128)} %all-reduce) | copy-start | bytes 772
  733.4 251.6 %copy-start.23 = (f32[4,384]{1,0:T(4,128)}, f32[4,384]{1,0:T(4,128)S(1)}, u32[]{:S(2)}) copy-start(f32[4,384]{1,0:T(4,128)S(1)} %multiply_multiply_fusion.1) | copy-start | bytes 18436
Sparse Core Ops, SparseCore 0:
  140.3 24.4 reduce-scatter.9
  255.1 10.8 reduce-scatter.11
  278.9 9.2 reduce-scatter.13
  327.2 9.2 reduce-scatter.15
  341.0 121.6 reduce-scatter.21
  468.0 123.9 reduce-scatter.23
  596.7 124.6 reduce-scatter.25
  726.2 124.1 reduce-scatter.19
  855.3 128.0 reduce-scatter.17
where the time goes:
time: 997 us; the launch traced here: 992 us
  waiting for transfers between devices  528 us (53%)
  blocking collectives  327 us (33%)
  matrix products  73.7 us (7%)
  other arithmetic  31.7 us (3%)
  local copies, waits for them, and re-layouts  16.3 us (2%)
  between operations  14.9 us (1%)
    reduce_scatter x1, waiting for transfers between devices, shards(): lax.psum_scatter(modulation_total, 'wide', scatter_dimension=0, tiled=True)  132 us
    reduce_scatter x1, waiting for transfers between devices, shards(): lax.psum_scatter(down_total, 'wide', scatter_dimension=1, tiled=True)  128 us
    reduce_scatter x1, waiting for transfers between devices, shards(): lax.psum_scatter(up_total, 'wide', scatter_dimension=0, tiled=True)  128 us
    reduce_scatter x1, waiting for transfers between devices, shards(): lax.psum_scatter(out_total, 'wide', scatter_dimension=1, tiled=True)  96.9 us
    psum x1, blocking collectives, shards(): lax.psum((jnp.sum(grad_modulation, axis=0), in_bias_part, jnp.sum(grad_at...  57.3 us
    psum x4, blocking collectives, feature_totals(): lax.psum((jnp.sum(first, axis=-1, keepdims=True), jnp.sum(second, axis=-1...  48 us
    all_gather x1, blocking collectives, shards(): lax.all_gather(modulation_weight, 'wide', axis=0, tiled=True)  36.9 us
    all_gather x1, blocking collectives, shards(): lax.all_gather(down_weight, 'wide', axis=1, tiled=True)  36.1 us
  transfers between devices with their start and end apart: 9, of which 7 were waited for; matrix products, arithmetic and copies ran while one was open for 5% of the time, Pallas kernels for 0%

commit v1 on v0

v1 whole, which is shorter than its diff:
```python
import functools
import math

import jax
import jax.numpy as jnp
from jax import lax
from jax.experimental import pallas as pl
from jax.experimental.pallas import tpu as pltpu
from jax.sharding import PartitionSpec as P

D = 384
HD = 64
LANES = 128
MESH = pl.DeviceIdType.MESH
VMEM_LIMIT = 60 * 1024 * 1024


EPS = 1e-06
GELU_K = 0.7978845608028654
GELU_A = 0.044715


def time_features(timesteps):
    half_width = D // 2
    frequencies = jnp.exp(
        jnp.arange(half_width, dtype=jnp.float32) * (-math.log(10000.0) / half_width)
    )
    angles = timesteps.astype(jnp.float32)[:, None] * frequencies[None, :]
    return jnp.concatenate([jnp.cos(angles), jnp.sin(angles)], axis=1)


def gelu_value(inputs):
    inner = GELU_K * (inputs + GELU_A * inputs * inputs * inputs)
    return 0.5 * inputs * (1.0 + jnp.tanh(inner))


def gelu_slope(inputs):
    inner = GELU_K * (inputs + GELU_A * inputs * inputs * inputs)
    tangent = jnp.tanh(inner)
    return 0.5 * (1.0 + tangent) + 0.5 * inputs * (1.0 - tangent * tangent) * GELU_K * (
        1.0 + 3.0 * GELU_A * inputs * inputs
    )


def silu_slope(inputs):
    sigmoid = jax.nn.sigmoid(inputs)
    return sigmoid * (1.0 + inputs * (1.0 - sigmoid))


def plane(wide):
    side = max(1, round((wide / 2) ** (1 / 3)))
    while wide % (side * side):
        side -= 1
    return wide // (side * side), side


class Place:
    def __init__(self, wide):
        self.deep, self.side = plane(wide)
        self.me = lax.axis_index("wide")
        self.core = lax.axis_index("narrow")
        self.z = self.me // (self.side * self.side)
        rest = self.me % (self.side * self.side)
        major, minor = rest // self.side, rest % self.side
        self.p = major + self.core * (minor - major)
        self.q = minor + self.core * (major - minor)
        self.p_stride = self.side + self.core * (1 - self.side)
        self.q_stride = 1 + self.core * (self.side - 1)

    def index(self, dz, dp, dq):
        return (
            ((self.z + dz) % self.deep) * (self.side * self.side)
            + ((self.p + dp) % self.side) * self.p_stride
            + ((self.q + dq) % self.side) * self.q_stride
        )

    def line_peers(self):
        return (
            [self.index(dz, 0, 0) for dz in range(1, self.deep)]
            + [self.index(0, dp, 0) for dp in range(1, self.side)]
            + [self.index(0, 0, dq) for dq in range(1, self.side)]
        )


def gather_kernel(
    wide, shard, tokens, upstream, biases,
    full, tokens_out, upstream_out, biases_out,
    send, recv, pair_send, pair_recv, swap_send, swap_recv, local,
):
    at = Place(wide)
    core, other = at.core, 1 - at.core
    barrier = pltpu.get_barrier_semaphore()
    peers = at.line_peers()
    for peer in peers:
        pl.semaphore_signal(barrier, 1, device_id=(peer, core), device_id_type=MESH)
    pl.semaphore_signal(barrier, 1, device_id=(at.me, other), device_id_type=MESH)
    pl.semaphore_wait(barrier, len(peers) + 1)
    waits = []
    count = 0

    def push(src, block, target):
        nonlocal count
        copy = pltpu.make_async_remote_copy(
            src, full.at[core, block], send.at[count], recv.at[block],
            device_id=(target, core), device_id_type=MESH,
        )
        copy.start()
        waits.append(copy)
        count += 1

    def share(src, block):
        copy = pltpu.make_async_remote_copy(
            src, full.at[core, block], pair_send.at[block], pair_recv.at[block],
            device_id=(at.me, other), device_id_type=MESH,
        )
        copy.start()
        waits.append(copy)

    def arrived(block):
        pltpu.make_async_copy(full.at[core, block], full.at[core, block], recv.at[block]).wait()

    for dz in range(1, at.deep):
        push(shard, at.me, at.index(dz, 0, 0))
    for dp in range(1, at.side):
        push(shard, at.me, at.index(0, dp, 0))
    for dq in range(1, at.side):
        push(shard, at.me, at.index(0, 0, dq))
    share(shard, at.me)
    half = tokens_out.shape[2]
    mine = pl.ds(pl.multiple_of(core * half, LANES), half)
    theirs = pl.ds(pl.multiple_of(other * half, LANES), half)
    for which, (src, dst) in enumerate(
        [(tokens.at[:, theirs], tokens_out), (upstream.at[:, theirs], upstream_out), (biases, biases_out)]
    ):
        copy = pltpu.make_async_remote_copy(
            src, dst.at[core], swap_send.at[which], swap_recv.at[which],
            device_id=(at.me, other), device_id_type=MESH,
        )
        copy.start()
        waits.append(copy)
    keeps = [
        pltpu.make_async_copy(src, dst, local.at[which])
        for which, (src, dst) in enumerate(
            [
                (tokens.at[:, mine], tokens_out.at[core]),
                (upstream.at[:, mine], upstream_out.at[core]),
                (biases, biases_out.at[core]),
                (shard, full.at[core, at.me]),
            ]
        )
    ]
    for keep in keeps:
        keep.start()
    for dz in range(1, at.deep):
        block = at.index(dz, 0, 0)
        arrived(block)
        for dp in range(1, at.side):
            push(full.at[core, block], block, at.index(0, dp, 0))
        for dq in range(1, at.side):
            push(full.at[core, block], block, at.index(0, 0, dq))
        share(full.at[core, block], block)
    for dz in range(at.deep):
        for dp in range(1, at.side):
            block = at.index(dz, dp, 0)
            arrived(block)
            for dq in range(1, at.side):
                push(full.at[core, block], block, at.index(0, 0, dq))
            share(full.at[core, block], block)
    for dz in range(at.deep):
        for dq in range(1, at.side):
            for dp in range(at.side):
                block = at.index(dz, dp, dq)
                arrived(block)
                share(full.at[core, block], block)
    for keep in keeps:
        keep.wait()
    for copy in waits:
        copy.wait_send()
    for block in range(wide):
        pltpu.make_async_copy(full.at[core, block], full.at[core, block], pair_recv.at[block]).wait()
    for which, (src, dst) in enumerate(
        [(tokens_out.at[core], None), (upstream_out.at[core], None), (biases_out.at[core], None)]
    ):
        pltpu.make_async_copy(src, src, swap_recv.at[which]).wait()


def gather_all(wide, shard, tokens, upstream, biases):
    rows, columns = shard.shape
    features, count = tokens.shape
    deep, side = plane(wide)
    sends = wide * (deep + 2 * side)
    vmem = pl.BlockSpec(memory_space=pltpu.VMEM)
    return pl.pallas_call(
        functools.partial(gather_kernel, wide),
        name="gather",
        out_shape=(
            jax.ShapeDtypeStruct((2, wide, rows, columns), shard.dtype),
            jax.ShapeDtypeStruct((2, features, count // 2), tokens.dtype),
            jax.ShapeDtypeStruct((2, features, count // 2), tokens.dtype),
            jax.ShapeDtypeStruct((2,) + biases.shape, biases.dtype),
        ),
        in_specs=[vmem] * 4,
        out_specs=(vmem,) * 4,
        scratch_shapes=[
            pltpu.SemaphoreType.DMA((sends,)),
            pltpu.SemaphoreType.DMA((wide,)),
            pltpu.SemaphoreType.DMA((wide,)),
            pltpu.SemaphoreType.DMA((wide,)),
            pltpu.SemaphoreType.DMA((3,)),
            pltpu.SemaphoreType.DMA((3,)),
            pltpu.SemaphoreType.DMA((4,)),
        ],
        compiler_params=pltpu.CompilerParams(
            collective_id=0, has_side_effects=True, vmem_limit_bytes=VMEM_LIMIT
        ),
    )(shard, tokens, upstream, biases)


def scatter_kernel(
    wide, parts, message, block_out, token_out,
    total, messages, block_half, token_half,
    from_pair, from_q, from_p, from_z, sums,
    send, pair_send, pair_recv, q_recv, p_recv, z_recv,
    note_send, note_recv, swap_send, swap_recv, local,
):
    at = Place(wide)
    core, other = at.core, 1 - at.core
    barrier = pltpu.get_barrier_semaphore()
    for step in range(wide):
        peer = (at.me + step) % wide
        if step:
            pl.semaphore_signal(barrier, 1, device_id=(peer, core), device_id_type=MESH)
        pl.semaphore_signal(barrier, 1, device_id=(peer, other), device_id_type=MESH)
    pl.semaphore_wait(barrier, 2 * wide - 1)
    waits = []

    deep, side = at.deep, at.side
    order = (
        [(dz, dp, dq) for dq in range(1, side) for dp in range(side) for dz in range(deep)]
        + [(dz, dp, 0) for dp in range(1, side) for dz in range(deep)]
        + [(dz, 0, 0) for dz in range(1, deep)]
        + [(0, 0, 0)]
    )
    for dz, dp, dq in order:
        block = at.index(dz, dp, dq)
        copy = pltpu.make_async_remote_copy(
            parts.at[other, block], from_pair.at[block], pair_send.at[block], pair_recv.at[block],
            device_id=(at.me, other), device_id_type=MESH,
        )
        copy.start()
        waits.append(copy)
    for step in range(wide):
        peer = (at.me + step) % wide
        for flip in range(2):
            if step == 0 and flip == 0:
                continue
            seat = core if flip == 0 else other
            copy = pltpu.make_async_remote_copy(
                message.at[seat], messages.at[at.me, core],
                note_send.at[step, flip], note_recv.at[at.me, core],
                device_id=(peer, seat), device_id_type=MESH,
            )
            copy.start()
            waits.append(copy)
    half = block_out.shape[0] // 2
    span = block_out.shape[1]
    columns = pl.ds(pl.multiple_of(core * span, LANES), span)
    mine = pl.ds(pl.multiple_of(core * half, 8), half)
    theirs = pl.ds(pl.multiple_of(other * half, 8), half)
    keeps = [pltpu.make_async_copy(message.at[core], messages.at[at.me, core], local.at[2])]
    for which, (src, dst) in enumerate([(block_out, block_half), (token_out, token_half)]):
        copy = pltpu.make_async_remote_copy(
            src.at[theirs], dst.at[:, columns], swap_send.at[which], swap_recv.at[which],
            device_id=(at.me, other), device_id_type=MESH,
        )
        copy.start()
        waits.append(copy)
        keeps.append(pltpu.make_async_copy(src.at[mine], dst.at[:, columns], local.at[which]))
    for keep in keeps:
        keep.start()

    def landed(ref, sem):
        pltpu.make_async_copy(ref, ref, sem).wait()

    f32 = jnp.float32
    for number, (dz, dp, dq) in enumerate(order):
        block = at.index(dz, dp, dq)
        landed(from_pair.at[block], pair_recv.at[block])
        value = parts[core, block].astype(f32) + from_pair[block].astype(f32)
        zs, ps = (at.z + dz) % deep, (at.p + dp) % side
        if dq == 0:
            for s in range(side - 1):
                landed(from_q.at[s, zs, ps], q_recv.at[s, zs, ps])
                value += from_q[s, zs, ps].astype(f32)
            if dp == 0:
                for s in range(side - 1):
                    landed(from_p.at[s, zs], p_recv.at[s, zs])
                    value += from_p[s, zs].astype(f32)
        if dq:
            target, slot, sem = (
                at.index(0, 0, dq), from_q.at[side - 1 - dq, zs, ps], q_recv.at[side - 1 - dq, zs, ps]
            )
        elif dp:
            target, slot, sem = (
                at.index(0, dp, 0), from_p.at[side - 1 - dp, zs], p_recv.at[side - 1 - dp, zs]
            )
        elif dz:
            target, slot, sem = at.index(dz, 0, 0), from_z.at[deep - 1 - dz], z_recv.at[deep - 1 - dz]
        else:
            for s in range(deep - 1):
                landed(from_z.at[s], z_recv.at[s])
                value += from_z[s].astype(f32)
            total[...] = value
            continue
        sums[block] = value.astype(jnp.bfloat16)
        copy = pltpu.make_async_remote_copy(
            sums.at[block], slot, send.at[number], sem,
            device_id=(target, core), device_id_type=MESH,
        )
        copy.start()
        waits.append(copy)
    for keep in keeps:
        keep.wait()
    for copy in waits:
        copy.wait_send()
    for step in range(wide):
        peer = (at.me + step) % wide
        if step:
            landed(messages.at[peer, core], note_recv.at[peer, core])
        landed(messages.at[peer, other], note_recv.at[peer, other])
    spare = pl.ds(pl.multiple_of(other * span, LANES), span)
    landed(block_half.at[:, spare], swap_recv.at[0])
    landed(token_half.at[:, spare], swap_recv.at[1])


def scatter_all(wide, parts, message, block_out, token_out):
    rows, columns = parts.shape[2:]
    features, count = block_out.shape
    deep, side = plane(wide)
    vmem = pl.BlockSpec(memory_space=pltpu.VMEM)
    bf, f32 = jnp.bfloat16, jnp.float32
    dma = pltpu.SemaphoreType.DMA
    return pl.pallas_call(
        functools.partial(scatter_kernel, wide),
        name="scatter",
        out_shape=(
            jax.ShapeDtypeStruct((rows, columns), f32),
            jax.ShapeDtypeStruct((wide,) + message.shape, bf),
            jax.ShapeDtypeStruct((features // 2, 2 * count), f32),
            jax.ShapeDtypeStruct((features // 2, 2 * count), f32),
        ),
        in_specs=[vmem] * 4,
        out_specs=(vmem,) * 4,
        scratch_shapes=[
            pltpu.VMEM((wide, rows, columns), bf),
            pltpu.VMEM((max(side - 1, 1), deep, side, rows, columns), bf),
            pltpu.VMEM((max(side - 1, 1), deep, rows, columns), bf),
            pltpu.VMEM((max(deep - 1, 1), rows, columns), bf),
            pltpu.VMEM((wide, rows, columns), bf),
            dma((wide,)),
            dma((wide,)),
            dma((wide,)),
            dma((max(side - 1, 1), deep, side)),
            dma((max(side - 1, 1), deep)),
            dma((max(deep - 1, 1),)),
            dma((wide, 2)),
            dma((wide, 2)),
            dma((2,)),
            dma((2,)),
            dma((3,)),
        ],
        compiler_params=pltpu.CompilerParams(
            collective_id=1, has_side_effects=True, vmem_limit_bytes=VMEM_LIMIT
        ),
    )(parts, message, block_out, token_out)


def norm_forward(values):
    average = jnp.mean(values, axis=-1, keepdims=True)
    centred = values - average
    inv_std = lax.rsqrt(jnp.mean(centred * centred, axis=-1, keepdims=True) + EPS)
    return centred * inv_std, inv_std


def norm_backward(grad_norm, normed, inv_std):
    first = jnp.mean(grad_norm, axis=-1, keepdims=True)
    second = jnp.mean(grad_norm * normed, axis=-1, keepdims=True)
    return inv_std * (grad_norm - first - normed * second)


def block_pass(
    tokens, upstream, full, modulation, bias_in, bias_out, bias_up, bias_down, own, sequence, width, hidden
):
    bf, f32 = jnp.bfloat16, jnp.float32
    features = 2 * width
    score_scale = HD ** (-0.5)
    join = lambda halves: jnp.concatenate([halves[0], halves[1]], axis=-1)
    up_full = join(full[:, :, :hidden])
    down_full = join(full[:, :, hidden : 2 * hidden])
    in_full = full[:, :, 2 * hidden : 2 * hidden + 3 * width].reshape(2, features, 3, width)
    out_full = join(full[:, :, 2 * hidden + 3 * width : 2 * hidden + 4 * width])
    in_full = jnp.transpose(in_full, (1, 2, 0, 3)).reshape(features, 3, features)
    in_bias = join(bias_in.reshape(2, 2, width))
    out_bias, up_bias, down_bias = join(bias_out), join(bias_up), join(bias_down)
    hidden_in = jnp.transpose(tokens).reshape(own, sequence, features)
    up_grad = jnp.transpose(upstream).reshape(own, sequence, features)
    shift_one, scale_one, gate_one, shift_two, scale_two, gate_two = [
        modulation[:, which][:, None, :] for which in range(6)
    ]
    head_shape = (own, sequence, features // HD, HD)
    dot = functools.partial(jnp.einsum, preferred_element_type=f32)
    normed_one, inv_one = norm_forward(hidden_in)
    modulated_one = (normed_one * (1.0 + scale_one) + shift_one).astype(bf)
    projected = dot("bsd,djf->bsjf", modulated_one, in_full)
    queries = (projected[:, :, 0] + in_bias[0]).astype(bf).reshape(head_shape)
    key_rows = projected[:, :, 1].astype(bf).reshape(head_shape)
    value_rows = (projected[:, :, 2] + in_bias[1]).astype(bf).reshape(head_shape)
    scores = dot("bshe,bthe->bhst", queries, key_rows) * score_scale
    log_total = jnp.log(jnp.sum(jnp.exp(scores), axis=-1, keepdims=True))
    weights_full = jnp.exp(scores - log_total)
    mixing = weights_full.astype(bf)
    attended = dot("bhst,bthe->bshe", mixing, value_rows).astype(bf).reshape(own, sequence, features)
    attention = dot("bsd,ed->bse", attended, out_full) + out_bias
    middle = hidden_in + gate_one * attention
    normed_two, inv_two = norm_forward(middle)
    modulated_two = (normed_two * (1.0 + scale_two) + shift_two).astype(bf)
    pre_act = dot("bsd,df->bsf", modulated_two, up_full) + up_bias
    activation = gelu_value(pre_act).astype(bf)
    feedforward = dot("bsf,df->bsd", activation, down_full) + down_bias
    block_output = middle + gate_two * feedforward
    gate_two_grad = jnp.sum(up_grad * feedforward, axis=1)
    grad_ff = gate_two * up_grad
    grad_ff_bf = grad_ff.astype(bf)
    down_total = dot("bsd,bsf->df", grad_ff_bf, activation)
    grad_pre = dot("bsd,df->bsf", grad_ff_bf, down_full) * gelu_slope(pre_act)
    grad_pre_bf = grad_pre.astype(bf)
    up_total = dot("bsd,bsf->df", modulated_two, grad_pre_bf)
    grad_mod_two = dot("bsf,df->bsd", grad_pre_bf, up_full)
    shift_two_grad = jnp.sum(grad_mod_two, axis=1)
    scale_two_grad = jnp.sum(grad_mod_two * normed_two, axis=1)
    grad_middle = up_grad + norm_backward(grad_mod_two * (1.0 + scale_two), normed_two, inv_two)
    gate_one_grad = jnp.sum(grad_middle * attention, axis=1)
    grad_att = gate_one * grad_middle
    grad_att_bf = grad_att.astype(bf)
    out_total = dot("bse,bsd->ed", grad_att_bf, attended)
    grad_attended = dot("bse,ed->bsd", grad_att_bf, out_full).astype(bf).reshape(head_shape)
    grad_mixing = dot("bshe,bthe->bhst", grad_attended, value_rows)
    row_dots = jnp.sum(weights_full * grad_mixing, axis=-1, keepdims=True)
    grad_scores = (weights_full * (grad_mixing - row_dots) * score_scale).astype(bf)
    flat_shape = (own, sequence, features)
    grad_queries = dot("bhst,bthe->bshe", grad_scores, key_rows).reshape(flat_shape)
    grad_keys = dot("bhst,bshe->bthe", grad_scores, queries).reshape(flat_shape)
    grad_values = dot("bhst,bshe->bthe", mixing, grad_attended).reshape(flat_shape)
    grad_proj = jnp.stack([grad_queries, grad_keys, grad_values], axis=2).astype(bf)
    in_total = dot("bsd,bsjf->djf", modulated_one, grad_proj)
    grad_mod_one = dot("bsjf,djf->bsd", grad_proj, in_full)
    shift_one_grad = jnp.sum(grad_mod_one, axis=1)
    scale_one_grad = jnp.sum(grad_mod_one * normed_one, axis=1)
    token_grads = grad_middle + norm_backward(grad_mod_one * (1.0 + scale_one), normed_one, inv_one)
    grad_modulation = jnp.stack(
        [shift_one_grad, scale_one_grad, gate_one_grad, shift_two_grad, scale_two_grad, gate_two_grad],
        axis=1,
    )
    split = lambda value: value.astype(bf).reshape(value.shape[:-1] + (2, value.shape[-1] // 2))
    parts = [
        jnp.concatenate(
            [
                split(up_total)[:, n],
                split(down_total)[:, n],
                split(in_total)[:, :, n].reshape(features, -1),
                split(out_total)[:, n],
            ],
            axis=1,
        )
        for n in range(2)
    ]
    sums = [
        jnp.sum(grad_queries, axis=(0, 1)),
        jnp.sum(grad_values, axis=(0, 1)),
        jnp.sum(grad_att, axis=(0, 1)),
        jnp.sum(grad_pre, axis=(0, 1)),
        jnp.sum(grad_ff, axis=(0, 1)),
    ]
    bias_sums = jnp.concatenate([s.reshape(2, -1) for s in sums], axis=1)
    transposed = lambda value: jnp.transpose(value.reshape(-1, features))
    return transposed(block_output), transposed(token_grads), jnp.stack(parts), grad_modulation, bias_sums


def codes(values):
    return jnp.concatenate([values // 256, values % 256]).astype(jnp.bfloat16)


def shards(
    latent_tokens,
    labels,
    timesteps,
    class_table,
    modulation_weight,
    modulation_bias,
    in_weight,
    in_bias,
    out_weight,
    out_bias,
    up_weight,
    up_bias,
    down_weight,
    down_bias,
    cotangent,
):
    bf, f32 = jnp.bfloat16, jnp.float32
    wide = lax.axis_size("wide")
    me, core = lax.axis_index("wide"), lax.axis_index("narrow")
    latent_count = labels.shape[0]
    own = latent_count // 2
    width = latent_tokens.shape[0]
    hidden = up_weight.shape[1]
    local_tokens = latent_tokens.shape[1]
    sequence = local_tokens // latent_count
    weight_scale = (local_tokens * wide) ** (-0.5)
    rows = up_weight.shape[0]

    ids = jnp.concatenate([codes(labels), codes(timesteps)])
    ids = jnp.pad(ids[None, :], ((0, rows - 1), (0, LANES - ids.shape[0])))
    shard = jnp.concatenate(
        [
            up_weight,
            jnp.transpose(down_weight),
            in_weight.reshape(rows, 3 * width),
            jnp.transpose(out_weight),
            modulation_weight.reshape(rows, 6 * width),
            ids,
        ],
        axis=1,
    )
    bias_parts = [in_bias.reshape(-1), out_bias, up_bias, down_bias, modulation_bias.reshape(-1)]
    biases = jnp.concatenate(bias_parts)
    pad = -biases.shape[0] % (8 * LANES)
    biases = jnp.pad(biases, (0, pad)).reshape(-1, LANES)
    full, tokens, upstream, both = gather_all(wide, shard, latent_tokens, cotangent, biases)
    ids_all = full[0, :, 0, -LANES:].astype(jnp.int32)
    pick = lambda n: ids_all[:, n * latent_count : (n + 1) * latent_count].reshape(-1)
    labels_all = pick(0) * 256 + pick(1)
    times_all = pick(2) * 256 + pick(3)
    class_ids = jnp.arange(class_table.shape[0], dtype=jnp.int32)
    every_hot = (labels_all[:, None] == class_ids[None, :]).astype(bf)
    condition_all = jnp.dot(every_hot, class_table, preferred_element_type=f32) + time_features(
        times_all
    )
    activated_all = jax.nn.silu(condition_all).astype(bf)
    first = me * latent_count + core * own
    condition = lax.dynamic_slice_in_dim(condition_all, first, own, 0)
    activated = lax.dynamic_slice_in_dim(activated_all, first, own, 0)

    full = full.reshape(2, rows * wide, -1)
    flat = both.reshape(2, -1)
    offset = 0
    halves = []
    for part in bias_parts:
        halves.append(flat[:, offset : offset + part.shape[0]])
        offset += part.shape[0]
    bias_in, bias_out, bias_up, bias_down, bias_mod = halves
    mod_at = 2 * hidden + 4 * width
    mod_full = full[:, :, mod_at : mod_at + 6 * width]
    modulation = jnp.einsum("bd,ndf->nbf", activated, mod_full, preferred_element_type=f32) + bias_mod[:, None]
    modulation = jnp.transpose(modulation.reshape(2, own, 6, width), (1, 2, 0, 3)).reshape(own, 6, 2 * width)

    block_output, token_grads, parts, grad_modulation, bias_sums = block_pass(
        tokens.reshape(2 * width, -1), upstream.reshape(2 * width, -1), full, modulation,
        bias_in, bias_out, bias_up, bias_down, own, sequence, width, hidden,
    )

    grad_modulation_bf = grad_modulation.astype(bf)
    by_half = jnp.transpose(grad_modulation_bf.reshape(own, 6, 2, width), (2, 0, 1, 3)).reshape(2, own, 6 * width)
    grad_activated = jnp.einsum("nbf,ndf->bd", by_half, mod_full, preferred_element_type=f32)
    condition_rows = (grad_activated * silu_slope(condition) * sequence ** (-0.5)).astype(bf)
    message = jnp.concatenate(
        [
            by_half.reshape(2, -1),
            jnp.broadcast_to(condition_rows.reshape(1, -1), (2, own * 2 * width)),
            bias_sums.astype(bf),
        ],
        axis=1,
    )
    used = message.shape[1]
    message = jnp.pad(message, ((0, 0), (0, -used % (16 * LANES)))).reshape(2, -1, LANES)
    total, messages, block_half, token_half = scatter_all(
        wide, parts.reshape(2, wide, rows, -1), message, block_output, token_grads
    )
    flat_notes = messages.reshape(wide * 2, -1)
    gm_all = flat_notes[:, : own * 6 * width].reshape(wide * latent_count, 6 * width)
    cond_all = flat_notes[:, own * 6 * width : own * 8 * width].reshape(wide * latent_count, 2 * width)
    sums = jnp.sum(flat_notes[:, own * 8 * width : used].astype(f32), axis=0) * weight_scale
    act_mine = lax.dynamic_slice_in_dim(activated_all, me * rows, rows, 1)
    mod_grads = jnp.einsum("bd,bf->df", act_mine, gm_all, preferred_element_type=f32) * weight_scale
    mod_bias_grads = jnp.sum(gm_all.astype(f32), axis=0) * weight_scale
    table_grads = jnp.einsum("bc,bd->cd", every_hot, cond_all, preferred_element_type=f32)
    condition_grads = lax.dynamic_slice_in_dim(cond_all, me * latent_count, latent_count, 0).astype(f32)
    total = total * weight_scale
    up_part = total[:, :hidden]
    down_part = jnp.transpose(total[:, hidden : 2 * hidden])
    in_part = total[:, 2 * hidden : 2 * hidden + 3 * width].reshape(rows, 3, width)
    out_part = jnp.transpose(total[:, 2 * hidden + 3 * width :])
    return (
        block_half,
        token_half,
        condition_grads,
        table_grads,
        mod_grads.reshape(rows, 6, width),
        mod_bias_grads.reshape(6, width),
        in_part,
        sums[: 2 * width].reshape(2, width),
        out_part,
        sums[2 * width : 3 * width],
        up_part,
        sums[3 * width : 3 * width + hidden],
        down_part,
        sums[3 * width + hidden :],
    )


def solution(mesh):
    return jax.shard_map(
        shards,
        mesh=mesh,
        in_specs=(
            P("narrow", "wide"),
            P("wide"),
            P("wide"),
            P(),
            P("wide", None, "narrow"),
            P(None, "narrow"),
            P("wide", None, "narrow"),
            P(None, "narrow"),
            P("narrow", "wide"),
            P("narrow"),
            P("wide", "narrow"),
            P("narrow"),
            P("narrow", "wide"),
            P("narrow"),
            P("narrow", "wide"),
        ),
        out_specs=(
            P("narrow", "wide"),
            P("narrow", "wide"),
            P("wide", None),
            P(),
            P("wide", None, "narrow"),
            P(None, "narrow"),
            P("wide", None, "narrow"),
            P(None, "narrow"),
            P("narrow", "wide"),
            P("narrow"),
            P("wide", "narrow"),
            P("narrow"),
            P("narrow", "wide"),
            P("narrow"),
        ),
        check_vma=False,
    )
```

time: 997 us -> 255 us (0.26)
  waiting for transfers between devices: 528 us -> 0 us
  blocking collectives: 327 us -> 0 us
  Pallas kernels: 0 us -> 84.7 us
  local copies, waits for them, and re-layouts: 16.3 us -> 80.5 us
  other arithmetic: 31.7 us -> 11.6 us
  between operations: 14.9 us -> 1.89 us
    reduce_scatter x9 -> x0, waiting for transfers between devices: 528 us -> none  [the longest x1 132 us: shards(): lax.psum_scatter(modulation_total, 'wide', scatter_dimension=0, tiled=True)]
    all_gather x10 -> x0, blocking collectives: 211 us -> none  [the longest x1 36.9 us: shards(): lax.all_gather(modulation_weight, 'wide', axis=0, tiled=True)]
    psum x5 -> x0, blocking collectives: 105 us -> none  [the longest x1 57.3 us: shards(): lax.psum((jnp.sum(grad_modulation, axis=0), in_bias_part, jnp.sum(grad_at...]
    pallas_call x0 -> x2, Pallas kernels: none -> 84.7 us  [the longest x1 45.7 us: gather_all(): pl.pallas_call(functools.partial(gather_kernel, wide), name='gather', out...]
    slice x3 -> x22, local copies, waits for them, and re-layouts: 2.38 us -> 16.4 us  [the longest x3 3.03 us: block_pass(): join = lambda halves: jnp.concatenate([halves[0], halves[1]], axis=-1)]
    unnamed x89 -> x127, local copies, waits for them, and re-layouts: 7.51 us -> 20.2 us
    reshape x2 -> x21, local copies, waits for them, and re-layouts: 3.09 us -> 15.3 us  [the longest x5 5.36 us: block_pass(): bias_sums = jnp.concatenate([s.reshape(2, -1) for s in sums], axis=1)]
    reduce_sum x9 -> x7, other arithmetic: 14.3 us -> 2.19 us  [the longest x1 1.53 us: block_pass(): jnp.sum(grad_ff, axis=(0, 1))]
  transfers between devices with their start and end apart: 9 -> 0, of which waited for: 7 -> 0; matrix products, arithmetic and copies ran while one was open for 5% -> 0% of each run, Pallas kernels for 0% -> 0%
where the time goes in v1:
time: 255 us; the launch traced here: 250 us
  Pallas kernels  84.7 us (33%)
  local copies, waits for them, and re-layouts  80.5 us (32%)
  matrix products  71 us (28%)
  other arithmetic  11.6 us (5%)
    pallas_call x1, Pallas kernels, gather_all(): pl.pallas_call(functools.partial(gather_kernel, wide), name='gather', out...  45.7 us
    pallas_call x1, Pallas kernels, scatter_all(): pl.pallas_call(functools.partial(scatter_kernel, wide), name='scatter', o...  38.9 us
    unnamed x127, local copies, waits for them, and re-layouts  20.2 us
    concatenate x4, local copies, waits for them, and re-layouts, block_pass(): jnp.concatenate([split(up_total)[:, n], split(down_total)[:, n], split(in...  8.84 us
    dot_general x1, matrix products, block_pass(): dot('bhst,bthe->bshe', grad_scores, key_rows).reshape(flat_shape)  6.99 us
    dot_general x1, matrix products, block_pass(): grad_keys = dot('bhst,bshe->bthe', grad_scores, queries).reshape(flat_shape)  6.4 us
    dot_general x1, matrix products, block_pass(): grad_pre = dot('bsd,df->bsf', grad_ff_bf, down_full) * gelu_slope(pre_act)  5.58 us
    dot_general x1, matrix products, block_pass(): dot('bhst,bshe->bthe', mixing, grad_attended).reshape(flat_shape)  5.41 us

profile of v1, /device:TPU:9, one launch (start us, length us, event | category | flops | bytes accessed | tf_op | source)
XLA Modules:
  0.0 249.6 jit_solution(8864627661055961516)
XLA Ops:
  1.5 0.9 copy.65
  3.4 1.5 concatenate.72.shard
  7.9 45.7 %gather.1 = (bf16[2,16,24,3584]{3,2,1,0:T(8,128)(2,1)}, f32[2,192,512]{2,1,0:T(8,128)}, f32[2,192,512]{2,1,0:T(8,128)}, f32[2,24,128]{2,1,0:T(8,128)}) custom-call(bf16[24,3584]{1,0:T(8,128)(2,1)} %concatenate.72.shard, f32[192,1024]{1,0:T(8,128)} %tokens.1, f32[192,1024]{1,0:T(8,128)} %upstream.1, f32[24,128]{1,0:T(8,128)} %pad_bitcast_fusion.1.biases), custom_call_target="tpu_custom_call" | custom-call | tf_op jit(solution)/shard_map/gather/pallas_call | solution.py:193
  55.0 0.9 multiply_convert_fusion.8
  57.4 1.9 fusion.17
  61.5 1.3 slice.246
  63.7 0.9 copy-done.3
  65.4 1.3 fusion.108
  66.7 2.3 copy.75
  70.7 2.0 add_convert_fusion.2
  73.0 3.5 %fusion.123 = f32[2,6,256,256]{2,3,1,0:T(8,128)} fusion(bf16[2,256,6,64]{1,3,2,0:T(8,128)(2,1)} %add_convert_fusion.2, bf16[2,256,6,64]{1,3,2,0:T(8,128)(2,1)S(1)} %bitcast.226), kind=kOutput, calls=%fused_computation.210 | convolution fusion | flops 100663296 | bytes 3932160 | tf_op jit(solution)/shard_map/bshe,bthe->bhst/dot_general | solution.py:418
  76.8 4.8 %convolution_convert_fusion = bf16[2,6,64,256]{3,2,1,0:T(8,128)(2,1)} fusion(f32[2,6,256,256]{2,3,1,0:T(8,128)} %fusion.123, f32[2,256,6,64]{1,3,2,0:T(8,128)S(1)} %bitcast.203, f32[6,64]{1,0:T(8,128)S(1)} %add.214), kind=kOutput, calls=%fused_computation.44 | convolution fusion | flops 104402176 | bytes 4326912 | tf_op jit(solution)/shard_map/bhst,bthe->bshe/dot_general | solution.py:422
  81.6 1.4 fusion.115
  83.7 1.2 slice_bitcast_fusion.5
  85.2 2.4 multiply_add_fusion.4
  88.0 0.9 slice_reduce_fusion.1
  88.9 2.8 %slice_bitcast_fusion.3 = (bf16[384,768]{1,0:T(8,128)(2,1)}, bf16[384,768]{1,0:T(8,128)(2,1)S(1)}, bf16[384,768]{1,0:T(8,128)(2,1)S(1)}, bf16[384,768]{1,0:T(8,128)(2,1)}) fusion(bf16[2,384,3584]{2,1,0:T(8,128)(2,1)} %bitcast.215), kind=kLoop, calls=%fused_computation.89 | loop fusion | bytes 4718592 | tf_op jit(solution)/shard_map/squeeze | solution.py:397
  91.8 0.9 copy-done.16
  92.6 2.7 %convolution_add_fusion = f32[2,256,1536]{2,1,0:T(8,128)} fusion(f32[1536]{0:T(1024)S(1)} %pad_maximum_fusion.4, bf16[384,768]{1,0:T(8,128)(2,1)S(1)} %get-tuple-element.76, bf16[384,768]{1,0:T(8,128)(2,1)S(1)} %get-tuple-element.77, f32[2,256,384]{2,1,0:T(8,128)S(1)} %get-tuple-element.124, f32[2,384]{1,0:T(2,128)S(1)} %copy-done.36, ...), kind=kOutput, calls=%fused_computation.5 | convolution fusion | flops 608108544 | bytes 5128192 | tf_op jit(solution)/shard_map/bsd,df->bsf/dot_general | solution.py:427
  95.3 1.1 copy.79
  96.5 5.6 %fusion.121 = (bf16[1536]{0:T(1024)(128)(2,1)}, bf16[2,256,1536]{2,1,0:T(8,128)(2,1)S(1)}) fusion(f32[2,256,1536]{2,1,0:T(8,128)} %convolution_add_fusion, bf16[384,768]{1,0:T(8,128)(2,1)} %get-tuple-element.78, bf16[384,768]{1,0:T(8,128)(2,1)} %get-tuple-element.75, f32[2,256,384]{2,1,0:T(8,128)} %bitcast.237, f32[2,384]{1,0:T(2,128)} %get-tuple-element.106), kind=kOutput, calls=%fused_computation.208 | convolution fusion | flops 622459392 | bytes 6690816 | tf_op jit(solution)/shard_map/bsd,df->bsf/dot_general | solution.py:435
  102.2 1.7 multiply_reduce_fusion.4
  104.4 1.0 copy-done.49
  105.4 3.1 %multiply_add_fusion.2 = (f32[2,256,384]{2,1,0:T(8,128)}, bf16[2,384]{1,0:T(2,128)(2,1)}, bf16[2,384]{1,0:T(2,128)(2,1)}, bf16[384]{0:T(512)(128)(2,1)}, f32[2,256,384]{2,1,0:T(8,128)S(1)}) fusion(f32[2,256,384]{2,1,0:T(8,128)S(1)} %get-tuple-element.124, f32[2,384]{1,0:T(2,128)S(1)} %copy-done.24, f32[512,384]{1,0:T(8,128)S(1)} %copy-done.10, ...), kind=kOutput, calls=%fused_computation.58 | convolution fusion | flops 616757376 | bytes 9853184 | tf_op jit(solution)/shard_map/bsf,df->bsd/dot_general | solution.py:429
  108.5 1.2 convolution_convert_fusion.1
  109.7 1.2 copy.84
  110.9 3.1 %fusion.71 = f32[2,6,256,256]{2,3,1,0:T(8,128)} fusion(bf16[2,256,6,64]{1,3,2,0:T(8,128)(2,1)S(1)} %bitcast.221, f32[2,256,6,64]{1,3,2,0:T(8,128)S(1)} %bitcast.204, f32[6,64]{1,0:T(8,128)} %copy-done.23), kind=kOutput, calls=%fused_computation.104 | convolution fusion | flops 101056512 | bytes 4326912 | tf_op jit(solution)/shard_map/bshe,bthe->bhst/dot_general | solution.py:447
  114.0 4.6 %fusion.7 = f32[2,6,256,256]{2,3,1,0:T(8,128)} fusion(bf16[2,256,6,64]{1,3,2,0:T(8,128)(2,1)} %add_convert_fusion.2, bf16[2,256,6,64]{1,3,2,0:T(8,128)(2,1)} %bitcast.227), kind=kOutput, calls=%fused_computation.13 | convolution fusion | flops 203689216 | bytes 3932160 | tf_op jit(solution)/shard_map/reduce_sum | solution.py:419
  118.7 7.0 %fusion.113 = (bf16[6,64]{1,0:T(8,128)(2,1)}, bf16[2,256,6,64]{1,3,2,0:T(8,128)(2,1)}) fusion(bf16[2,256,6,64]{1,3,2,0:T(8,128)(2,1)S(1)} %bitcast.228, f32[2,6,256,256]{2,3,1,0:T(8,128)} %fusion.7, f32[2,6,256,256]{2,3,1,0:T(8,128)} %fusion.71), kind=kOutput, calls=%fused_computation.204 | convolution fusion | flops 104991616 | bytes 7078656 | tf_op jit(solution)/shard_map/bhst,bthe->bshe/dot_general | solution.py:451
  125.7 6.4 %fusion.33 = bf16[2,6,64,256]{3,2,1,0:T(8,128)(2,1)} fusion(bf16[2,256,6,64]{1,3,2,0:T(8,128)(2,1)S(1)} %copy-done.9, f32[2,6,256,256]{2,3,1,0:T(8,128)} %fusion.7, f32[2,6,256,256]{2,3,1,0:T(8,128)} %fusion.71), kind=kOutput, calls=%fused_computation.42 | convolution fusion | flops 104795392 | bytes 7077888 | tf_op jit(solution)/shard_map/bhst,bshe->bthe/dot_general | solution.py:452
  132.1 5.4 %fusion.112 = (bf16[6,64]{1,0:T(8,128)(2,1)}, bf16[2,256,6,64]{1,3,2,0:T(8,128)(2,1)}) fusion(bf16[2,256,6,64]{1,3,2,0:T(8,128)(2,1)S(1)} %bitcast.222, f32[2,6,256,256]{2,3,1,0:T(8,128)} %fusion.123), kind=kOutput, calls=%fused_computation.203 | convolution fusion | flops 104205184 | bytes 3932928 | tf_op jit(solution)/shard_map/bhst,bshe->bthe/dot_general | solution.py:453
  137.5 3.1 %multiply_reduce_fusion.1 = (f32[2,256]{1,0:T(2,128)S(1)}, bf16[2,384]{1,0:T(2,128)(2,1)}, f32[2,256]{1,0:T(2,128)S(1)}, bf16[2,384]{1,0:T(2,128)(2,1)}, f32[2,256,384]{2,1,0:T(8,128)S(1)}) fusion(f32[2,256,384]{2,1,0:T(8,128)S(1)} %bitcast.197, f32[2,256]{1,0:T(2,128)S(1)} %rsqrt.22, f32[2,256]{1,0:T(2,128)S(1)} %div.65, ...), kind=kOutput, calls=%fused_computation.57 | convolution fusion | flops 456324608 | bytes 4438016 | tf_op jit(solution)/shard_map/bsjf,djf->bsd/dot_general | solution.py:456
  141.0 1.2 copy.119
  146.3 2.0 fusion.46
  149.1 1.3 reshape.353
  150.4 1.3 reshape.354
  151.7 1.3 reshape.355
  153.1 1.3 reshape.356
  155.1 1.1 copy.98
  156.2 1.5 multiply_reduce_fusion.2
  159.9 2.1 bitcast_convert_fusion
  162.1 0.9 fusion.111
  163.8 1.4 concatenate.83
  165.2 3.6 %fusion.11 = bf16[384,1536]{1,0:T(8,128)(2,1)S(1)} fusion(f32[2,256,384]{2,1,0:T(8,128)} %bitcast.238, f32[2,384]{1,0:T(2,128)S(1)} %copy-done.25, f32[2,256,1536]{2,1,0:T(8,128)} %convolution_add_fusion), kind=kOutput, calls=%fused_computation.23 | convolution fusion | flops 612040704 | bytes 5114880 | tf_op jit(solution)/shard_map/bsd,bsf->df/dot_general | solution.py:434
  169.4 1.6 fusion.109
  171.0 0.9 copy.121
  171.9 1.9 fusion.10
  173.9 2.9 %reshape.347 = bf16[384,2,768]{2,1,0:T(2,128)(2,1)S(1)} reshape(bf16[384,1536]{1,0:T(8,128)(2,1)} %fusion.10) | data formatting | bytes 2359296 | tf_op jit(solution)/shard_map/reshape | solution.py:464
  176.8 2.6 %fusion.110 = (bf16[384,1,768]{2,1,0:T(2,128)(2,1)S(1)}, bf16[384,1,768]{2,1,0:T(2,128)(2,1)}) fusion(bf16[384,2,768]{2,1,0:T(2,128)(2,1)S(1)} %reshape.347), kind=kLoop, calls=%fused_computation.201 | loop fusion | bytes 2359296 | tf_op jit(solution)/shard_map/slice | solution.py:468
  179.4 0.9 copy.120
  180.3 2.5 concatenate.85
  183.6 2.1 copy.126
  185.8 2.5 concatenate.88
  188.2 0.9 copy.125
  189.1 2.1 copy.124
  191.3 2.5 %concatenate.90 = bf16[1,16,24,2304]{3,2,1,0:T(8,128)(2,1)S(1)} concatenate(bf16[1,16,24,768]{3,2,1,0:T(8,128)(2,1)} %bitcast.220, bf16[1,16,24,768]{3,2,1,0:T(8,128)(2,1)} %bitcast.218, bf16[1,16,24,576]{3,2,1,0:T(8,128)(2,1)} %concatenate.88, bf16[1,16,24,192]{3,2,1,0:T(8,128)(2,1)} %bitcast.235), dimensions={3} | concatenate | bytes 3538944 | tf_op jit(solution)/shard_map/concatenate | solution.py:466
  193.8 2.1 pad_maximum_fusion.parts
  195.9 2.3 copy.118
  198.1 38.9 %scatter.1 = (f32[24,2304]{1,0:T(8,128)}, bf16[16,2,48,128]{3,2,1,0:T(8,128)(2,1)}, f32[192,1024]{1,0:T(8,128)}, f32[192,1024]{1,0:T(8,128)}) custom-call(bf16[2,16,24,2304]{3,2,1,0:T(8,128)(2,1)} %pad_maximum_fusion.parts, bf16[2,48,128]{2,1,0:T(8,128)(2,1)} %bitcast.243, f32[384,512]{1,0:T(8,128)} %bitcast.205, f32[384,512]{1,0:T(8,128)} %bitcast.202), custom_call_target="tpu_custom_call" | custom-call | tf_op jit(solution)/shard_map/scatter/pallas_call | solution.py:343
  237.1 1.2 copy.134
  238.4 1.1 convolution_multiply_fusion.1
  240.3 1.6 fusion.70
  247.4 0.9 copy.144
  248.3 0.9 copy.145
  (210 shorter events, 32.2 us)
Async XLA Ops:
  0.6 54.4 %copy-start = (bf16[1001,384]{1,0:T(8,128)(2,1)S(1)}, bf16[1001,384]{1,0:T(8,128)(2,1)}, u32[]{:S(2)}) copy-start(bf16[1001,384]{1,0:T(8,128)(2,1)} %param.18) | copy-start | bytes 2306308
  55.0 5.0 %copy-start.41 = (s32[64]{0:T(128)}, s32[64]{0:T(128)S(1)}, u32[]{:S(2)}) copy-start(s32[64]{0:T(128)S(1)} %add.199) | copy-start | bytes 772
  56.0 4.1 %copy-start.33 = (bf16[64,384]{1,0:T(8,128)(2,1)}, bf16[64,384]{1,0:T(8,128)(2,1)S(1)}, u32[]{:S(2)}) copy-start(bf16[64,384]{1,0:T(8,128)(2,1)S(1)} %get-tuple-element.122) | copy-start | bytes 147460
  56.7 0.6 copy-start.21
  57.4 3.4 %copy-start.2 = (f32[2,192,512]{2,1,0:T(8,128)S(1)}, f32[2,192,512]{2,1,0:T(8,128)}, u32[]{:S(2)}) copy-start(f32[2,192,512]{2,1,0:T(8,128)} %get-tuple-element.22) | copy-start | bytes 2359300
  60.1 0.7 copy-start.26
  60.1 80.5 %copy-start.22 = (f32[2,384]{1,0:T(2,128)}, f32[2,384]{1,0:T(2,128)S(1)}, u32[]{:S(2)}) copy-start(f32[2,384]{1,0:T(2,128)S(1)} %get-tuple-element.110) | copy-start | bytes 9220
  63.7 0.9 copy-start.3
  72.7 3.7 %copy-start.5 = (f32[2,256,1,384]{3,1,2,0:T(8,128)S(1)}, f32[2,256,1,384]{3,1,2,0:T(8,128)}, u32[]{:S(2)}) copy-start(f32[2,256,1,384]{3,1,2,0:T(8,128)} %get-tuple-element.81) | copy-start | bytes 2359300
  72.7 4.0 %copy-start.32 = (f32[384]{0:T(512)S(1)}, f32[384]{0:T(512)}, u32[]{:S(2)}) copy-start(f32[384]{0:T(512)} %get-tuple-element.72) | copy-start | bytes 4612
  72.9 8.7 %copy-start.7 = (bf16[2,256,1,384]{1,3,0,2:T(8,128)(2,1)}, bf16[2,256,1,384]{1,3,0,2:T(8,128)(2,1)S(1)}, u32[]{:S(2)}) copy-start(bf16[2,256,1,384]{1,3,0,2:T(8,128)(2,1)S(1)} %copy.76) | copy-start | bytes 1179652
  76.8 6.2 %copy-start.23 = (f32[6,64]{1,0:T(8,128)}, f32[6,64]{1,0:T(8,128)S(1)}, u32[]{:S(2)}) copy-start(f32[6,64]{1,0:T(8,128)S(1)} %add.214) | copy-start | bytes 4612
  87.7 4.9 %copy-start.36 = (f32[2,384]{1,0:T(2,128)S(1)}, f32[2,384]{1,0:T(2,128)}, u32[]{:S(2)}) copy-start(f32[2,384]{1,0:T(2,128)} %get-tuple-element.107) | copy-start | bytes 9220
  87.7 4.9 %copy-start.38 = (f32[2,384]{1,0:T(2,128)S(1)}, f32[2,384]{1,0:T(2,128)}, u32[]{:S(2)}) copy-start(f32[2,384]{1,0:T(2,128)} %get-tuple-element.108) | copy-start | bytes 9220
  87.8 7.6 %copy-start.27 = (f32[2,256]{1,0:T(2,128)}, f32[2,256]{1,0:T(2,128)S(1)}, u32[]{:S(2)}) copy-start(f32[2,256]{1,0:T(2,128)S(1)} %broadcast_multiply_fusion.7) | copy-start | bytes 6148
  88.0 7.3 %copy-start.43 = (f32[2,256]{1,0:T(2,128)}, f32[2,256]{1,0:T(2,128)S(1)}, u32[]{:S(2)}) copy-start(f32[2,256]{1,0:T(2,128)S(1)} %add_rsqrt_fusion) | copy-start | bytes 6148
  91.7 0.9 copy-start.16
  91.7 3.6 %copy-start.18 = (bf16[384,768]{1,0:T(8,128)(2,1)}, bf16[384,768]{1,0:T(8,128)(2,1)S(1)}, u32[]{:S(2)}) copy-start(bf16[384,768]{1,0:T(8,128)(2,1)S(1)} %get-tuple-element.77) | copy-start | bytes 1769476
  91.7 3.6 %copy-start.4 = (f32[2,192,512]{2,1,0:T(8,128)S(1)}, f32[2,192,512]{2,1,0:T(8,128)}, u32[]{:S(2)}) copy-start(f32[2,192,512]{2,1,0:T(8,128)} %get-tuple-element.25) | copy-start | bytes 2359300
  96.5 5.6 %copy-start.17 = (bf16[384,768]{1,0:T(8,128)(2,1)S(1)}, bf16[384,768]{1,0:T(8,128)(2,1)}, u32[]{:S(2)}) copy-start(bf16[384,768]{1,0:T(8,128)(2,1)} %copy-done.16) | copy-start | bytes 1769476
  96.5 5.6 %copy-start.19 = (bf16[384,768]{1,0:T(8,128)(2,1)S(1)}, bf16[384,768]{1,0:T(8,128)(2,1)}, u32[]{:S(2)}) copy-start(bf16[384,768]{1,0:T(8,128)(2,1)} %copy-done.18) | copy-start | bytes 1769476
  96.5 5.6 %copy-start.28 = (f32[2,256]{1,0:T(2,128)S(1)}, f32[2,256]{1,0:T(2,128)}, u32[]{:S(2)}) copy-start(f32[2,256]{1,0:T(2,128)} %copy-done.27) | copy-start | bytes 6148
  96.5 5.6 %copy-start.39 = (f32[2,384]{1,0:T(2,128)S(1)}, f32[2,384]{1,0:T(2,128)}, u32[]{:S(2)}) copy-start(f32[2,384]{1,0:T(2,128)} %get-tuple-element.108) | copy-start | bytes 9220
  96.5 5.6 %copy-start.44 = (f32[2,256]{1,0:T(2,128)S(1)}, f32[2,256]{1,0:T(2,128)}, u32[]{:S(2)}) copy-start(f32[2,256]{1,0:T(2,128)} %copy-done.43) | copy-start | bytes 6148
  102.1 1.8 copy-start.50
  102.1 1.8 copy-start.34
  102.1 1.8 copy-start.35
  102.1 1.9 copy-start.10
  102.2 1.9 copy-start.13
  102.2 2.1 copy-start.14
  102.2 2.2 copy-start.15
  102.2 2.2 copy-start.24
  102.2 3.2 %copy-start.49 = (f32[2,256,1536]{2,1,0:T(8,128)S(1)}, f32[2,256,1536]{2,1,0:T(8,128)}, u32[]{:S(2)}) copy-start(f32[2,256,1536]{2,1,0:T(8,128)} %convolution_add_fusion) | copy-start | bytes 9437188
  114.0 4.6 %copy-start.8 = (bf16[2,256,1,384]{1,3,0,2:T(8,128)(2,1)S(1)}, bf16[2,256,1,384]{1,3,0,2:T(8,128)(2,1)}, u32[]{:S(2)}) copy-start(bf16[2,256,1,384]{1,3,0,2:T(8,128)(2,1)} %copy-done.7) | copy-start | bytes 1179652
  118.7 7.0 %copy-start.9 = (bf16[2,256,6,64]{1,3,2,0:T(8,128)(2,1)S(1)}, bf16[2,256,6,64]{1,3,2,0:T(8,128)(2,1)}, u32[]{:S(2)}) copy-start(bf16[2,256,6,64]{1,3,2,0:T(8,128)(2,1)} %add_convert_fusion.2) | copy-start | bytes 1179652
  132.1 5.4 %copy-start.47 = (bf16[2,256,6,64]{1,3,2,0:T(8,128)(2,1)S(1)}, bf16[2,256,6,64]{1,3,2,0:T(8,128)(2,1)}, u32[]{:S(2)}) copy-start(bf16[2,256,6,64]{1,3,2,0:T(8,128)(2,1)} %get-tuple-element.97) | copy-start | bytes 1179652
  132.1 5.4 %copy-start.48 = (bf16[2,6,64,256]{3,2,1,0:T(8,128)(2,1)S(1)}, bf16[2,6,64,256]{3,2,1,0:T(8,128)(2,1)}, u32[]{:S(2)}) copy-start(bf16[2,6,64,256]{3,2,1,0:T(8,128)(2,1)} %fusion.33) | copy-start | bytes 1179652
  137.5 3.1 %copy-start.30 = (f32[2,256]{1,0:T(2,128)}, f32[2,256]{1,0:T(2,128)S(1)}, u32[]{:S(2)}) copy-start(f32[2,256]{1,0:T(2,128)S(1)} %rsqrt.22) | copy-start | bytes 6148
  137.5 3.1 %copy-start.31 = (f32[2,256]{1,0:T(2,128)}, f32[2,256]{1,0:T(2,128)S(1)}, u32[]{:S(2)}) copy-start(f32[2,256]{1,0:T(2,128)S(1)} %div.65) | copy-start | bytes 6148
  140.6 4.8 %copy-start.46 = (bf16[2,384]{1,0:T(2,128)(2,1)S(1)}, bf16[2,384]{1,0:T(2,128)(2,1)}, u32[]{:S(2)}) copy-start(bf16[2,384]{1,0:T(2,128)(2,1)} %get-tuple-element.58) | copy-start | bytes 4612
  142.2 17.1 %copy-start.6 = (bf16[2,6,64,256]{3,2,1,0:T(8,128)(2,1)S(1)}, bf16[2,6,64,256]{3,2,1,0:T(8,128)(2,1)}, u32[]{:S(2)}) copy-start(bf16[2,6,64,256]{3,2,1,0:T(8,128)(2,1)} %convolution_convert_fusion) | copy-start | bytes 1179652
  162.1 3.1 %copy-start.25 = (f32[2,384]{1,0:T(2,128)S(1)}, f32[2,384]{1,0:T(2,128)}, u32[]{:S(2)}) copy-start(f32[2,384]{1,0:T(2,128)} %get-tuple-element.106) | copy-start | bytes 9220
  169.3 2.6 %copy-start.29 = (f32[2,256]{1,0:T(2,128)S(1)}, f32[2,256]{1,0:T(2,128)}, u32[]{:S(2)}) copy-start(f32[2,256]{1,0:T(2,128)} %copy-done.27) | copy-start | bytes 6148
  169.3 2.6 %copy-start.37 = (f32[2,384]{1,0:T(2,128)S(1)}, f32[2,384]{1,0:T(2,128)}, u32[]{:S(2)}) copy-start(f32[2,384]{1,0:T(2,128)} %get-tuple-element.107) | copy-start | bytes 9220
  169.4 2.6 %copy-start.40 = (f32[2,384]{1,0:T(2,128)S(1)}, f32[2,384]{1,0:T(2,128)}, u32[]{:S(2)}) copy-start(f32[2,384]{1,0:T(2,128)} %get-tuple-element.108) | copy-start | bytes 9220
  169.4 2.5 %copy-start.45 = (f32[2,256]{1,0:T(2,128)S(1)}, f32[2,256]{1,0:T(2,128)}, u32[]{:S(2)}) copy-start(f32[2,256]{1,0:T(2,128)} %copy-done.43) | copy-start | bytes 6148
  169.4 2.5 %copy-start.51 = (bf16[2,256,1536]{2,1,0:T(8,128)(2,1)S(1)}, bf16[2,256,1536]{2,1,0:T(8,128)(2,1)}, u32[]{:S(2)}) copy-start(bf16[2,256,1536]{2,1,0:T(8,128)(2,1)} %copy-done.50) | copy-start | bytes 4718596
  198.1 42.2 %copy-start.42 = (s32[64]{0:T(128)S(1)}, s32[64]{0:T(128)}, u32[]{:S(2)}) copy-start(s32[64]{0:T(128)} %copy-done.41) | copy-start | bytes 772
  237.1 6.2 %copy-start.20 = (f32[24,2304]{1,0:T(8,128)S(1)}, f32[24,2304]{1,0:T(8,128)}, u32[]{:S(2)}) copy-start(f32[24,2304]{1,0:T(8,128)} %get-tuple-element.29) | copy-start | bytes 663556
  237.1 10.3 %copy-start.12 = (f32[192,1024]{1,0:T(8,128)S(1)}, f32[192,1024]{1,0:T(8,128)}, u32[]{:S(2)}) copy-start(f32[192,1024]{1,0:T(8,128)} %get-tuple-element.150) | copy-start | bytes 2359300
  238.3 10.0 %copy-start.11 = (f32[192,1024]{1,0:T(8,128)S(1)}, f32[192,1024]{1,0:T(8,128)}, u32[]{:S(2)}) copy-start(f32[192,1024]{1,0:T(8,128)} %get-tuple-element.151) | copy-start | bytes 2359300
  240.3 8.9 %copy-start.1 = (bf16[1001,384]{1,0:T(8,128)(2,1)S(1)}, bf16[1001,384]{1,0:T(8,128)(2,1)}, u32[]{:S(2)}) copy-start(bf16[1001,384]{1,0:T(8,128)(2,1)} %param.18) | copy-start | bytes 2306308

commit v2 on v1

--- a/solution.py
+++ b/solution.py
@@ -388,102 +388,223 @@
     return inv_std * (grad_norm - first - normed * second)
 
 
+def block_kernel(
+    own, sequence, width, hidden,
+    tokens, upstream, full, modulation, bias_in, bias_out, bias_up, bias_down,
+    block_out, token_out, parts, grad_mod, sum_heads, sum_out, sum_up, sum_down,
+    hid, upg, normed, inv, mod_bf, normed_two, inv_two, mod_two, gff, attention, feed, gmod,
+    qkv, att_heads, att, weights, gatt_heads, gatt, gproj_heads, gproj,
+):
+    bf, f32 = jnp.bfloat16, jnp.float32
+    features = 2 * width
+    heads = features // HD
+    per_half = heads // 2
+    count = own * sequence
+    score_scale = HD ** (-0.5)
+    rows = LANES if sequence % LANES == 0 else sequence
+    blocks = count // rows
+    chunk = 256 if hidden % 256 == 0 else hidden
+    chunks = hidden // chunk
+    in_at, out_at = 2 * hidden, 2 * hidden + 3 * width
+
+    def dot(a, b, left, right):
+        return lax.dot_general(a, b, (((left,), (right,)), ((), ())), preferred_element_type=f32)
+
+    def total(value):
+        return jnp.sum(value, axis=0, keepdims=True)
+
+    grad_mod[...] = jnp.zeros_like(grad_mod)
+    sum_heads[...] = jnp.zeros_like(sum_heads)
+    sum_out[...] = jnp.zeros_like(sum_out)
+    sum_down[...] = jnp.zeros_like(sum_down)
+    feed[...] = jnp.zeros_like(feed)
+    gmod[...] = jnp.zeros_like(gmod)
+
+    def span(r):
+        return pl.ds(pl.multiple_of(r * rows, rows), rows), (r * rows) // sequence
+
+    @pl.loop(0, blocks)
+    def _(r):
+        at, b = span(r)
+        values = jnp.transpose(tokens[:, at])
+        hid[at, :] = values
+        unit, scale = norm_forward(values)
+        normed[at, :] = unit
+        inv[at, :] = scale
+        mod_bf[at, :] = (unit * (1.0 + modulation[b, 1:2, :]) + modulation[b, 0:1, :]).astype(bf)
+        up = jnp.transpose(upstream[:, at])
+        upg[at, :] = up
+        grad = modulation[b, 5:6, :] * up
+        gff[at, :] = grad.astype(bf)
+        sum_down[...] += total(grad)
+
+    @pl.loop(0, blocks)
+    def _(r):
+        at, b = span(r)
+        for n in range(2):
+            out = dot(mod_bf[at, :], full[n, :, in_at:out_at], 1, 0)
+            for j in range(3):
+                for h in range(per_half):
+                    low = j * width + h * HD
+                    piece = out[:, low : low + HD]
+                    if j != 1:
+                        piece = piece + bias_in[j // 2, n * per_half + h]
+                    qkv[j, n * per_half + h, at, :] = piece.astype(bf)
+
+    @pl.loop(0, own * heads)
+    def _(i):
+        b, h = i // heads, i % heads
+        at = pl.ds(pl.multiple_of(b * sequence, sequence), sequence)
+        scores = dot(qkv[0, h, at, :], qkv[1, h, at, :], 1, 1) * score_scale
+        log_total = jnp.log(jnp.sum(jnp.exp(scores), axis=-1, keepdims=True))
+        mix = jnp.exp(scores - log_total)
+        weights[i] = mix
+        att_heads[h, at, :] = dot(mix.astype(bf), qkv[2, h, at, :], 1, 0).astype(bf)
+
+    for n in range(2):
+        att[n] = jnp.concatenate([att_heads[n * per_half + h] for h in range(per_half)], axis=1)
+
+    @pl.loop(0, blocks)
+    def _(r):
+        at, b = span(r)
+        result = bias_out[...] + sum(
+            dot(att[n, at, :], full[n, :, out_at : out_at + width], 1, 1) for n in range(2)
+        )
+        attention[at, :] = result
+        middle = hid[at, :] + modulation[b, 2:3, :] * result
+        hid[at, :] = middle
+        unit, scale = norm_forward(middle)
+        normed_two[at, :] = unit
+        inv_two[at, :] = scale
+        mod_two[at, :] = (unit * (1.0 + modulation[b, 4:5, :]) + modulation[b, 3:4, :]).astype(bf)
+
+    @pl.loop(0, 2 * chunks)
+    def _(i):
+        n, c = i // chunks, i % chunks
+        at = pl.ds(pl.multiple_of(c * chunk, chunk), chunk)
+        down_at = pl.ds(pl.multiple_of(hidden + c * chunk, chunk), chunk)
+        up_w, down_w = full[n, :, at], full[n, :, down_at]
+        pre = dot(mod_two[...], up_w, 1, 0) + bias_up[n, :, at]
+        tangent = jnp.tanh(GELU_K * (pre + GELU_A * pre * pre * pre))
+        act = (0.5 * pre * (1.0 + tangent)).astype(bf)
+        slope = 0.5 * (1.0 + tangent) + 0.5 * pre * (1.0 - tangent * tangent) * GELU_K * (
+            1.0 + 3.0 * GELU_A * pre * pre
+        )
+        feed[...] += dot(act, down_w, 1, 1)
+        parts[n, :, down_at] = dot(gff[...], act, 0, 0).astype(bf)
+        grad = dot(gff[...], down_w, 1, 0) * slope
+        sum_up[n, :, at] = total(grad)
+        grad_bf = grad.astype(bf)
+        parts[n, :, at] = dot(mod_two[...], grad_bf, 0, 0).astype(bf)
+        gmod[...] += dot(grad_bf, up_w, 1, 1)
+
+    @pl.loop(0, blocks)
+    def _(r):
+        at, b = span(r)
+        ff = feed[at, :] + bias_down[...]
+        up = upg[at, :]
+        block_out[:, at] = jnp.transpose(hid[at, :] + modulation[b, 5:6, :] * ff)
+        grad_mod[b, 5:6, :] += total(up * ff)
+        grad, unit = gmod[at, :], normed_two[at, :]
+        grad_mod[b, 3:4, :] += total(grad)
+        grad_mod[b, 4:5, :] += total(grad * unit)
+        middle = up + norm_backward(grad * (1.0 + modulation[b, 4:5, :]), unit, inv_two[at, :])
+        upg[at, :] = middle
+        grad_mod[b, 2:3, :] += total(middle * attention[at, :])
+        grad_att = modulation[b, 2:3, :] * middle
+        sum_out[...] += total(grad_att)
+        grad_bf = grad_att.astype(bf)
+        gatt[at, :] = grad_bf
+        for n in range(2):
+            out = dot(grad_bf, full[n, :, out_at : out_at + width], 1, 0).astype(bf)
+            for h in range(per_half):
+                gatt_heads[n * per_half + h, at, :] = out[:, h * HD : (h + 1) * HD]
+
+    @pl.loop(0, own * heads)
+    def _(i):
+        b, h = i // heads, i % heads
+        at = pl.ds(pl.multiple_of(b * sequence, sequence), sequence)
+        mix, grad_out = weights[i], gatt_heads[h, at, :]
+        grad_mix = dot(grad_out, qkv[2, h, at, :], 1, 1)
+        dots = jnp.sum(mix * grad_mix, axis=-1, keepdims=True)
+        grad_scores = (mix * (grad_mix - dots) * score_scale).astype(bf)
+        grad_q = dot(grad_scores, qkv[1, h, at, :], 1, 0)
+        grad_k = dot(grad_scores, qkv[0, h, at, :], 0, 0)
+        grad_v = dot(mix.astype(bf), grad_out, 0, 0)
+        gproj_heads[0, h, at, :] = grad_q.astype(bf)
+        gproj_heads[1, h, at, :] = grad_k.astype(bf)
+        gproj_heads[2, h, at, :] = grad_v.astype(bf)
+        sum_heads[0, h] += total(grad_q)
+        sum_heads[1, h] += total(grad_v)
+
+    for n in range(2):
+        gproj[n] = jnp.concatenate(
+            [gproj_heads[j, n * per_half + h] for j in range(3) for h in range(per_half)], axis=1
+        )
+        parts[n, :, in_at:] = jnp.concatenate(
+            [dot(mod_bf[...], gproj[n], 0, 0), dot(gatt[...], att[n], 0, 0)], axis=1
+        ).astype(bf)
+
+    @pl.loop(0, blocks)
+    def _(r):
+        at, b = span(r)
+        grad = sum(dot(gproj[n, at, :], full[n, :, in_at:out_at], 1, 1) for n in range(2))
+        unit = normed[at, :]
+        grad_mod[b, 0:1, :] += total(grad)
+        grad_mod[b, 1:2, :] += total(grad * unit)
+        back = norm_backward(grad * (1.0 + modulation[b, 1:2, :]), unit, inv[at, :])
+        token_out[:, at] = jnp.transpose(upg[at, :] + back)
+
+
 def block_pass(
     tokens, upstream, full, modulation, bias_in, bias_out, bias_up, bias_down, own, sequence, width, hidden
 ):
     bf, f32 = jnp.bfloat16, jnp.float32
     features = 2 * width
-    score_scale = HD ** (-0.5)
-    join = lambda halves: jnp.concatenate([halves[0], halves[1]], axis=-1)
-    up_full = join(full[:, :, :hidden])
-    down_full = join(full[:, :, hidden : 2 * hidden])
-    in_full = full[:, :, 2 * hidden : 2 * hidden + 3 * width].reshape(2, features, 3, width)
-    out_full = join(full[:, :, 2 * hidden + 3 * width : 2 * hidden + 4 * width])
-    in_full = jnp.transpose(in_full, (1, 2, 0, 3)).reshape(features, 3, features)
-    in_bias = join(bias_in.reshape(2, 2, width))
-    out_bias, up_bias, down_bias = join(bias_out), join(bias_up), join(bias_down)
-    hidden_in = jnp.transpose(tokens).reshape(own, sequence, features)
-    up_grad = jnp.transpose(upstream).reshape(own, sequence, features)
-    shift_one, scale_one, gate_one, shift_two, scale_two, gate_two = [
-        modulation[:, which][:, None, :] for which in range(6)
-    ]
-    head_shape = (own, sequence, features // HD, HD)
-    dot = functools.partial(jnp.einsum, preferred_element_type=f32)
-    normed_one, inv_one = norm_forward(hidden_in)
-    modulated_one = (normed_one * (1.0 + scale_one) + shift_one).astype(bf)
-    projected = dot("bsd,djf->bsjf", modulated_one, in_full)
-    queries = (projected[:, :, 0] + in_bias[0]).astype(bf).reshape(head_shape)
-    key_rows = projected[:, :, 1].astype(bf).reshape(head_shape)
-    value_rows = (projected[:, :, 2] + in_bias[1]).astype(bf).reshape(head_shape)
-    scores = dot("bshe,bthe->bhst", queries, key_rows) * score_scale
-    log_total = jnp.log(jnp.sum(jnp.exp(scores), axis=-1, keepdims=True))
-    weights_full = jnp.exp(scores - log_total)
-    mixing = weights_full.astype(bf)
-    attended = dot("bhst,bthe->bshe", mixing, value_rows).astype(bf).reshape(own, sequence, features)
-    attention = dot("bsd,ed->bse", attended, out_full) + out_bias
-    middle = hidden_in + gate_one * attention
-    normed_two, inv_two = norm_forward(middle)
-    modulated_two = (normed_two * (1.0 + scale_two) + shift_two).astype(bf)
-    pre_act = dot("bsd,df->bsf", modulated_two, up_full) + up_bias
-    activation = gelu_value(pre_act).astype(bf)
-    feedforward = dot("bsf,df->bsd", activation, down_full) + down_bias
-    block_output = middle + gate_two * feedforward
-    gate_two_grad = jnp.sum(up_grad * feedforward, axis=1)
-    grad_ff = gate_two * up_grad
-    grad_ff_bf = grad_ff.astype(bf)
-    down_total = dot("bsd,bsf->df", grad_ff_bf, activation)
-    grad_pre = dot("bsd,df->bsf", grad_ff_bf, down_full) * gelu_slope(pre_act)
-    grad_pre_bf = grad_pre.astype(bf)
-    up_total = dot("bsd,bsf->df", modulated_two, grad_pre_bf)
-    grad_mod_two = dot("bsf,df->bsd", grad_pre_bf, up_full)
-    shift_two_grad = jnp.sum(grad_mod_two, axis=1)
-    scale_two_grad = jnp.sum(grad_mod_two * normed_two, axis=1)
-    grad_middle = up_grad + norm_backward(grad_mod_two * (1.0 + scale_two), normed_two, inv_two)
-    gate_one_grad = jnp.sum(grad_middle * attention, axis=1)
-    grad_att = gate_one * grad_middle
-    grad_att_bf = grad_att.astype(bf)
-    out_total = dot("bse,bsd->ed", grad_att_bf, attended)
-    grad_attended = dot("bse,ed->bsd", grad_att_bf, out_full).astype(bf).reshape(head_shape)
-    grad_mixing = dot("bshe,bthe->bhst", grad_attended, value_rows)
-    row_dots = jnp.sum(weights_full * grad_mixing, axis=-1, keepdims=True)
-    grad_scores = (weights_full * (grad_mixing - row_dots) * score_scale).astype(bf)
-    flat_shape = (own, sequence, features)
-    grad_queries = dot("bhst,bthe->bshe", grad_scores, key_rows).reshape(flat_shape)
-    grad_keys = dot("bhst,bshe->bthe", grad_scores, queries).reshape(flat_shape)
-    grad_values = dot("bhst,bshe->bthe", mixing, grad_attended).reshape(flat_shape)
-    grad_proj = jnp.stack([grad_queries, grad_keys, grad_values], axis=2).astype(bf)
-    in_total = dot("bsd,bsjf->djf", modulated_one, grad_proj)
-    grad_mod_one = dot("bsjf,djf->bsd", grad_proj, in_full)
-    shift_one_grad = jnp.sum(grad_mod_one, axis=1)
-    scale_one_grad = jnp.sum(grad_mod_one * normed_one, axis=1)
-    token_grads = grad_middle + norm_backward(grad_mod_one * (1.0 + scale_one), normed_one, inv_one)
-    grad_modulation = jnp.stack(
-        [shift_one_grad, scale_one_grad, gate_one_grad, shift_two_grad, scale_two_grad, gate_two_grad],
+    heads = features // HD
+    count = own * sequence
+    bias_in = jnp.transpose(bias_in.reshape(2, 2, width), (1, 0, 2)).reshape(2, heads, 1, HD)
+    vmem = pl.BlockSpec(memory_space=pltpu.VMEM)
+    sds = jax.ShapeDtypeStruct
+    wide_f32, wide_bf = pltpu.VMEM((count, features), f32), pltpu.VMEM((count, features), bf)
+    column = pltpu.VMEM((count, 1), f32)
+    by_head = pltpu.VMEM((heads, count, HD), bf)
+    by_head_three = pltpu.VMEM((3, heads, count, HD), bf)
+    block_out, token_out, parts, grad_mod, sum_heads, sum_out, sum_up, sum_down = pl.pallas_call(
+        functools.partial(block_kernel, own, sequence, width, hidden),
+        name="block",
+        out_shape=(
+            sds((features, count), f32),
+            sds((features, count), f32),
+            sds((2, features, 2 * hidden + 4 * width), bf),
+            sds((own, 6, features), f32),
+            sds((2, heads, 1, HD), f32),
+            sds((1, features), f32),
+            sds((2, 1, hidden), f32),
+            sds((1, features), f32),
+        ),
+        in_specs=[vmem] * 8,
+        out_specs=(vmem,) * 8,
+        scratch_shapes=[
+            wide_f32, wide_f32, wide_f32, column, wide_bf, wide_f32, column, wide_bf, wide_bf, wide_f32,
+            wide_f32, wide_f32,
+            by_head_three, by_head, pltpu.VMEM((2, count, width), bf),
+            pltpu.VMEM((own * heads, sequence, sequence), f32),
+            by_head, wide_bf, by_head_three, pltpu.VMEM((2, count, 3 * width), bf),
+        ],
+        compiler_params=pltpu.CompilerParams(vmem_limit_bytes=VMEM_LIMIT),
+    )(
+        tokens, upstream, full, modulation, bias_in, bias_out.reshape(1, -1),
+        bias_up.reshape(2, 1, hidden), bias_down.reshape(1, -1),
+    )
+    by_half = lambda value: value.reshape(2, -1)
+    bias_sums = jnp.concatenate(
+        [
+            by_half(sum_heads[0]), by_half(sum_heads[1]), by_half(sum_out), by_half(sum_up), by_half(sum_down),
+        ],
         axis=1,
     )
-    split = lambda value: value.astype(bf).reshape(value.shape[:-1] + (2, value.shape[-1] // 2))
-    parts = [
-        jnp.concatenate(
-            [
-                split(up_total)[:, n],
-                split(down_total)[:, n],
-                split(in_total)[:, :, n].reshape(features, -1),
-                split(out_total)[:, n],
-            ],
-            axis=1,
-        )
-        for n in range(2)
-    ]
-    sums = [
-        jnp.sum(grad_queries, axis=(0, 1)),
-        jnp.sum(grad_values, axis=(0, 1)),
-        jnp.sum(grad_att, axis=(0, 1)),
-        jnp.sum(grad_pre, axis=(0, 1)),
-        jnp.sum(grad_ff, axis=(0, 1)),
-    ]
-    bias_sums = jnp.concatenate([s.reshape(2, -1) for s in sums], axis=1)
-    transposed = lambda value: jnp.transpose(value.reshape(-1, features))
-    return transposed(block_output), transposed(token_grads), jnp.stack(parts), grad_modulation, bias_sums
+    return block_out, token_out, parts, grad_mod, bias_sums
 
 
 def codes(values):

time: 255 us -> 159 us (0.62); the launches traced: 250 us -> 158 us
  matrix products: 71 us -> 6.08 us
  local copies, waits for them, and re-layouts: 80.5 us -> 21 us
  Pallas kernels: 84.7 us -> 123 us
  other arithmetic: 11.6 us -> 7.2 us
    dot_general x18 -> x0, matrix products: 58.8 us -> none  [the longest x1 6.99 us: block_pass(): dot('bhst,bthe->bshe', grad_scores, key_rows).reshape(flat_shape)]
    pallas_call x0 -> x1, Pallas kernels: none -> 38 us  [block_pass(): pl.pallas_call(functools.partial(block_kernel, own, sequence, width, hidd...]
    slice x14 -> x1, local copies, waits for them, and re-layouts: 14.4 us -> 0.03 us  [block_pass(): sum_heads[1]]
    unnamed x127 -> x17, local copies, waits for them, and re-layouts: 20.2 us -> 7.31 us
    reshape x9 -> x8, local copies, waits for them, and re-layouts: 12.4 us -> 2.93 us  [the longest x1 0.68 us: block_pass(): jnp.transpose(bias_in.reshape(2, 2, width), (1, 0, 2))]
    concatenate x4 -> x0, local copies, waits for them, and re-layouts: 8.84 us -> none  [block_pass(): jnp.concatenate([split(up_total)[:, n], split(down_total)[:, n], split(in...]
    reduce_sum x1 -> x0, matrix products: 4.63 us -> none  [block_pass(): log_total = jnp.log(jnp.sum(jnp.exp(scores), axis=-1, keepdims=True))]
    squeeze x4 -> x0, local copies, waits for them, and re-layouts: 4.21 us -> none  [block_pass(): join = lambda halves: jnp.concatenate([halves[0], halves[1]], axis=-1)]
where the time goes in v2:
time: 159 us; the launch traced here: 158 us
  Pallas kernels  123 us (77%)
  local copies, waits for them, and re-layouts  21 us (13%)
  other arithmetic  7.2 us (5%)
  matrix products  6.08 us (4%)
    pallas_call x1, Pallas kernels, gather_all(): pl.pallas_call(functools.partial(gather_kernel, wide), name='gather', out...  45.7 us
    pallas_call x1, Pallas kernels, scatter_all(): pl.pallas_call(functools.partial(scatter_kernel, wide), name='scatter', o...  38.8 us
    pallas_call x1, Pallas kernels, block_pass(): pl.pallas_call(functools.partial(block_kernel, own, sequence, width, hidd...  38 us
    unnamed x17, local copies, waits for them, and re-layouts  7.31 us
    another operation x5, other arithmetic  3.48 us

profile of v2, /device:TPU:9, one launch (start us, length us, event | category | flops | bytes accessed | tf_op | source)
XLA Modules:
  0.0 157.7 jit_solution(11799659655544292797)
XLA Ops:
  0.7 0.8 reshape.169
  1.5 0.7 fusion.27
  2.2 0.1 maximum_bitcast_fusion
  2.3 0.8 reshape.170
  3.1 0.8 concatenate.25
  3.8 0.6 pad_bitcast_fusion.1.biases
  4.5 0.8 copy.37
  5.2 0.1 reshape.167
  5.3 0.9 copy.38
  6.3 0.1 reshape.168
  6.4 1.5 concatenate.24.shard
  7.9 45.7 %gather.1 = (bf16[2,16,24,3584]{3,2,1,0:T(8,128)(2,1)}, f32[2,192,512]{2,1,0:T(8,128)}, f32[2,192,512]{2,1,0:T(8,128)}, f32[2,24,128]{2,1,0:T(8,128)}) custom-call(bf16[24,3584]{1,0:T(8,128)(2,1)} %concatenate.24.shard, f32[192,1024]{1,0:T(8,128)} %tokens.1, f32[192,1024]{1,0:T(8,128)} %upstream.1, f32[24,128]{1,0:T(8,128)} %pad_bitcast_fusion.1.biases), custom_call_target="tpu_custom_call" | custom-call | tf_op jit(solution)/shard_map/gather/pallas_call | solution.py:193
  53.6 0.8 slice_convert_fusion
  54.4 0.1 fusion.20
  54.5 0.1 convert_element_type.47
  54.6 0.1 add.76
  54.7 0.8 copy.59
  55.4 0.1 reshape.178
  55.5 0.7 reshape.179.bias_in
  56.2 0.1 fusion.29
  56.3 0.6 reshape.182.bias_down
  56.9 0.6 reshape.180.bias_out
  57.6 0.1 slice.111
  57.6 0.6 reshape.181.bias_up
  58.2 0.3 multiply_cosine_fusion
  58.6 0.3 multiply_convert_fusion
  58.9 1.8 %fusion = f32[2,2,1152]{2,1,0:T(2,128)S(1)} fusion(bf16[2,384,3584]{2,1,0:T(8,128)(2,1)} %bitcast.54, f32[2,1152]{1,0:T(2,128)S(1)} %slice.108, bf16[64,384]{1,0:T(8,128)(2,1)S(1)} %get-tuple-element.90, s32[]{:T(128)S(6)} %select_n.33), kind=kOutput, calls=%fused_computation.2 | convolution fusion | flops 3543552 | bytes 1798660 | tf_op jit(solution)/shard_map/bd,ndf->nbf/dot_general | solution.py:685
  60.7 0.1 reshape.176
  60.8 0.7 reshape.198.modulation
  61.5 38.0 %block.1 = (f32[384,512]{1,0:T(8,128)}, f32[384,512]{1,0:T(8,128)}, bf16[2,384,2304]{2,1,0:T(8,128)(2,1)}, f32[2,6,384]{2,1,0:T(8,128)}, f32[2,6,1,64]{3,2,1,0:T...) custom-call(f32[384,512]{1,0:T(8,128)} %bitcast.61, f32[384,512]{1,0:T(8,128)} %bitcast.62, ...), custom_call_target="tpu_custom_call" | custom-call | tf_op jit(solution)/shard_map/block/pallas_call | solution.py:573
  99.6 0.7 convert_reduce_fusion.3
  100.3 0.1 reshape.186
  100.3 0.7 convert_reduce_fusion.2
  101.0 0.1 reshape.188
  101.1 0.7 convert.37
  101.9 0.1 reshape_squeeze.9
  101.9 0.1 reshape_squeeze.8
  102.0 0.7 convert.39
  102.7 0.7 convert_element_type.49
  103.5 0.1 reshape.184
  103.6 0.1 reshape.185
  103.7 2.0 %fusion.13 = bf16[2,384]{1,0:T(2,128)(2,1)S(1)} fusion(bf16[2,2,1152]{2,1,0:T(2,128)(2,1)S(1)} %reshape.185, bf16[2,384,3584]{2,1,0:T(8,128)(2,1)} %bitcast.56, f32[64,384]{1,0:T(8,128)S(1)} %get-tuple-element.91, s32[]{:T(128)S(6)} %select_n.33), kind=kOutput, calls=%fused_computation.10 | convolution fusion | flops 3546624 | bytes 1783300 | tf_op jit(solution)/shard_map/nbf,ndf->bd/dot_general | solution.py:695
  105.7 0.1 reshape_reshape.3
  105.9 0.1 concatenate.27
  106.0 0.6 copy.58
  106.6 38.8 %scatter.1 = (f32[24,2304]{1,0:T(8,128)}, bf16[16,2,48,128]{3,2,1,0:T(8,128)(2,1)}, f32[192,1024]{1,0:T(8,128)}, f32[192,1024]{1,0:T(8,128)}) custom-call(bf16[2,16,24,2304]{3,2,1,0:T(8,128)(2,1)} %bitcast.57, bf16[2,48,128]{2,1,0:T(8,128)(2,1)} %bitcast.66, f32[384,512]{1,0:T(8,128)} %get-tuple-element.40.block_out, f32[384,512]{1,0:T(8,128)} %get-tuple-element.41.token_out), custom_call_target="tpu_custom_call" | custom-call | tf_op jit(solution)/shard_map/scatter/pallas_call | solution.py:343
  145.5 1.1 broadcast_multiply_fusion
  146.6 0.7 slice_bitcast_fusion.1
  147.3 0.7 slice_bitcast_fusion
  147.9 0.1 reshape.194
  148.0 0.6 copy.46
  148.7 1.1 copy.57
  149.8 0.7 slice.96
  150.5 0.6 fusion.30
  151.1 0.7 slice.123
  151.8 0.1 reshape.192
  151.9 0.6 dynamic-slice_convert_fusion
  152.5 0.3 convolution_multiply_fusion
  152.8 0.7 mul.118
  153.5 0.1 reshape.193
  153.6 0.7 copy.45
  154.3 1.6 %fusion.16 = f32[1001,384]{1,0:T(8,128)} fusion(bf16[64,384]{1,0:T(8,128)(2,1)S(1)} %reshape.191, s32[64]{0:T(128)S(1)} %add.76), kind=kOutput, calls=%fused_computation.14 | convolution fusion | flops 49265216 | bytes 1586944 | tf_op jit(solution)/shard_map/bc,bd->cd/dot_general | solution.py:717
  155.9 0.9 copy.63
  156.8 0.9 copy.64
  (28 shorter events, 0.3 us)
Async XLA Ops:
  0.6 57.9 %copy-start = (bf16[1001,384]{1,0:T(8,128)(2,1)S(1)}, bf16[1001,384]{1,0:T(8,128)(2,1)}, u32[]{:S(2)}) copy-start(bf16[1001,384]{1,0:T(8,128)(2,1)} %param.18) | copy-start | bytes 2306308
  145.5 10.5 %copy-start.2 = (f32[192,1024]{1,0:T(8,128)S(1)}, f32[192,1024]{1,0:T(8,128)}, u32[]{:S(2)}) copy-start(f32[192,1024]{1,0:T(8,128)} %get-tuple-element.108) | copy-start | bytes 2359300
  145.5 11.3 %copy-start.1 = (f32[192,1024]{1,0:T(8,128)S(1)}, f32[192,1024]{1,0:T(8,128)}, u32[]{:S(2)}) copy-start(f32[192,1024]{1,0:T(8,128)} %get-tuple-element.109) | copy-start | bytes 2359300
